TPU v7x, 512 devices: a whole 4x4x16 slice. The times are simulated.
512 devices in a mesh: dp: 8 (over y, core), expert: 64 (over x, z).
Axes of the slice: x: 4, y: 4, z: 16, core: 2. Of those that a mesh axis runs over, the one named last changes fastest.
Arguments:
- tokens: bfloat16 [65536, 4096], P(('dp', 'expert')), may hold values from -6 to 6
- expert_ids: int32 [65536, 2], P(('dp', 'expert')), may hold values from 0 to 63, as said below
- gate_values: float32 [65536, 2], P(('dp', 'expert')), may hold values from 0.2 to 1
- w_gate: bfloat16 [4096, 14336], P('dp', 'expert'), may hold values from -0.09375 to 0.09375
- w_up: bfloat16 [4096, 14336], P('dp', 'expert'), may hold values from -0.09375 to 0.09375
- w_down: bfloat16 [14336, 4096], P('expert', 'dp'), may hold values from -0.046875 to 0.046875
- target: bfloat16 [65536, 4096], P(('dp', 'expert')), may hold values from -6 to 6
Outputs:
- token_grad: bfloat16 [65536, 4096], P(('dp', 'expert'))
- gate_grad: bfloat16 [4096, 14336], P('dp', 'expert')
- up_grad: bfloat16 [4096, 14336], P('dp', 'expert')
Inputs may be any that keep to these rules, and one draw needn't show every extreme that they name: `expert_ids`: A token's two expert ids differ, and no token names two experts below 1. Among the 128 tokens of one device each expert below 1 is named by 1 to 3 tokens, and in every draw some device names each of them exactly 3 times.
All inputs are finite; a program needn't handle non-finite values.
Results may differ from a plain program's by a relative error of at most 0.008.
Values may be sent and summed in bfloat16 or wider, within the bound.
A program may use at most 64 MiB of HBM per device.

v0:
```python
import jax
import jax.numpy as jnp
from jax import lax
from jax.sharding import PartitionSpec as P

EXPERTS = 1


def contract_last(matrix_a, matrix_b):
    return lax.dot_general(
        matrix_a, matrix_b, (((1,), (1,)), ((), ())), preferred_element_type=jnp.float32
    )


def rounded_terms(column_blocks, grad_blocks):
    terms = jnp.einsum(
        "krd,krh->kdh", column_blocks, grad_blocks, preferred_element_type=jnp.float32
    )
    terms = lax.optimization_barrier(terms.astype(jnp.bfloat16))
    return jnp.sum(terms.astype(jnp.float32), axis=0)


def spread_rows(rows, group_size, capacity, features):
    flat = rows.reshape(EXPERTS, 1, capacity * features)
    wide = jnp.broadcast_to(flat, (EXPERTS, group_size, capacity * features))
    return wide.reshape(EXPERTS * group_size * capacity, features)


def fold_group(rows, group_size, capacity, features):
    shaped = rows.reshape(EXPERTS, group_size, capacity * features).astype(jnp.float32)
    return jnp.sum(shaped, axis=1).reshape(EXPERTS * capacity, features)


def shards(tokens, expert_ids, gate_values, w_gate, w_up, w_down, target):
    devices_along = lax.axis_size("expert")
    group_size = devices_along // EXPERTS
    tok_rows = tokens.shape[0]
    features = tokens.shape[1]
    hid_local = w_gate.shape[1]
    capacity = max(2, 3 * tok_rows // 128)
    slot_total = EXPERTS * capacity
    flat_ids = expert_ids.reshape(-1)
    pair_count = flat_ids.shape[0]
    window = flat_ids < EXPERTS
    onehot = (flat_ids[:, None] == jnp.arange(EXPERTS, dtype=jnp.int32)[None, :]).astype(jnp.int32)
    slot_index = jnp.sum((jnp.cumsum(onehot, axis=0) - onehot) * onehot, axis=1)
    position = jnp.where(window, flat_ids * capacity + slot_index, slot_total)
    owning = jnp.arange(pair_count, dtype=jnp.int32) // 2
    slot_token = jnp.zeros((slot_total + 1,), jnp.int32).at[position].set(owning)[:slot_total]
    slot_live = jnp.zeros((slot_total + 1,), jnp.bool_).at[position].set(True)[:slot_total]
    slot_gate = (
        jnp.zeros((slot_total + 1,), jnp.float32)
        .at[position]
        .set(gate_values.reshape(-1))[:slot_total]
    )
    safe_pairs = jnp.minimum(position, slot_total - 1).reshape(tok_rows, 2)
    live_pairs = window.reshape(tok_rows, 2)

    def pick(table, column):
        return jnp.where(live_pairs[:, column : column + 1], table[safe_pairs[:, column]], 0.0)

    outgoing = jnp.where(slot_live[:, None], tokens[slot_token], jnp.zeros((), tokens.dtype))
    outgoing = spread_rows(outgoing, group_size, capacity, features)
    received = lax.all_to_all(outgoing, "expert", split_axis=0, concat_axis=0, tiled=True)
    rows_count = received.shape[0]
    full_gate, full_up, full_down = (
        lax.all_gather(w_gate, "dp", axis=0, tiled=True),
        lax.all_gather(w_up, "dp", axis=0, tiled=True),
        lax.all_gather(w_down, "dp", axis=1, tiled=True),
    )
    gate_pre = jnp.dot(received, full_gate, preferred_element_type=jnp.float32)
    up_pre = jnp.dot(received, full_up, preferred_element_type=jnp.float32)
    sigmoid_gate = jax.nn.sigmoid(gate_pre)
    activated = sigmoid_gate * gate_pre
    hidden = (activated * up_pre).astype(jnp.bfloat16)
    partial_out = jnp.dot(hidden, full_down, preferred_element_type=jnp.float32).astype(
        jnp.bfloat16
    )
    returned_out = lax.all_to_all(partial_out, "expert", split_axis=0, concat_axis=0, tiled=True)
    expert_out = fold_group(returned_out, group_size, capacity, features)
    combined = gate_values[:, 0:1] * pick(expert_out, 0) + gate_values[:, 1:2] * pick(expert_out, 1)
    residual = combined - target.astype(jnp.float32)
    outgoing_grad = jnp.where(
        slot_live[:, None], slot_gate[:, None] * residual[slot_token], 0.0
    ).astype(jnp.bfloat16)
    outgoing_grad = spread_rows(outgoing_grad, group_size, capacity, features)
    cotangent = lax.all_to_all(outgoing_grad, "expert", split_axis=0, concat_axis=0, tiled=True)
    grad_hidden = contract_last(cotangent, full_down)
    derivative = sigmoid_gate * (1.0 + gate_pre * (1.0 - sigmoid_gate))
    grad_gate_pre = (grad_hidden * up_pre * derivative).astype(jnp.bfloat16)
    grad_up_pre = (grad_hidden * activated).astype(jnp.bfloat16)
    row_part = (
        contract_last(grad_gate_pre, full_gate) + contract_last(grad_up_pre, full_up)
    ).astype(jnp.bfloat16)
    back_rows = lax.all_to_all(row_part, "expert", split_axis=0, concat_axis=0, tiled=True)
    row_grad = fold_group(back_rows, group_size, capacity, features)
    token_grad = (pick(row_grad, 0) + pick(row_grad, 1)).astype(jnp.bfloat16)
    shard_columns = lax.all_to_all(received, "dp", split_axis=1, concat_axis=0, tiled=True)
    shard_width = shard_columns.shape[1]
    dp_count = lax.axis_size("dp")
    every_gate, every_up = (
        lax.all_gather(grad_gate_pre, "dp", axis=0, tiled=True),
        lax.all_gather(grad_up_pre, "dp", axis=0, tiled=True),
    )
    column_blocks = shard_columns.reshape(dp_count, rows_count, shard_width)
    gate_sum = rounded_terms(column_blocks, every_gate.reshape(dp_count, rows_count, hid_local))
    up_sum = rounded_terms(column_blocks, every_up.reshape(dp_count, rows_count, hid_local))
    return (token_grad, gate_sum.astype(jnp.bfloat16), up_sum.astype(jnp.bfloat16))


def solution(mesh):
    placed = (
        P(("dp", "expert"), None),
        P(("dp", "expert"), None),
        P(("dp", "expert"), None),
        P("dp", "expert"),
        P("dp", "expert"),
        P("expert", "dp"),
        P(("dp", "expert"), None),
    )
    return jax.shard_map(
        shards,
        mesh=mesh,
        in_specs=placed,
        out_specs=(P(("dp", "expert"), None), P("dp", "expert"), P("dp", "expert")),
        check_vma=False,
    )
```

profile of v0, /device:TPU:6, one launch (start us, length us, event | category | flops | bytes accessed | tf_op | source)
XLA Modules:
  0.0 524.1 jit_solution(15885397472876217078)
XLA Ops:
  14.0 2.4 broadcast_in_dim.87
  16.4 18.8 %all-to-all-start = ((bf16[64,3,4096]{2,1,0:T(4,128)(2,1)}), bf16[64,3,4096]{2,1,0:T(4,128)(2,1)S(1)}, u32[]{:S(2)}, u32[]{:S(2)}) async-start(bf16[64,3,4096]{2,1,0:T(4,128)(2,1)} %broadcast_in_dim.87), calls=%async_computation | async-start | bytes 4194304 | tf_op jit(solution)/shard_map/all_to_all | solution.py:64
  36.7 95.8 %all-to-all-done = bf16[64,3,4096]{2,1,0:T(4,128)(2,1)S(1)} async-done(((bf16[64,3,4096]{2,1,0:T(4,128)(2,1)}), bf16[64,3,4096]{2,1,0:T(4,128)(2,1)S(1)}, u32[]{:S(2)}, u32[]{:S(2)}) %all-to-all-start) | async-done | bytes 1572896 | tf_op jit(solution)/shard_map/all_to_all | solution.py:64
  132.5 2.5 all_to_all.37
  135.0 2.7 fusion.16
  137.8 3.4 fusion.15
  141.2 3.4 convolution_convert_fusion
  144.5 4.1 all_to_all.38
  148.6 8.6 %all-to-all-start.1 = ((bf16[64,3,4096]{2,1,0:T(4,128)(2,1)}), bf16[64,3,4096]{2,1,0:T(4,128)(2,1)}, u32[]{:S(2)}, u32[]{:S(2)}) async-start(bf16[64,3,4096]{2,1,0:T(4,128)(2,1)} %all_to_all.38), calls=%async_computation.1 | async-start | bytes 4194304 | tf_op jit(solution)/shard_map/all_to_all | solution.py:79
  159.5 94.7 %all-to-all-done.1 = bf16[64,3,4096]{2,1,0:T(4,128)(2,1)} async-done(((bf16[64,3,4096]{2,1,0:T(4,128)(2,1)}), bf16[64,3,4096]{2,1,0:T(4,128)(2,1)}, u32[]{:S(2)}, u32[]{:S(2)}) %all-to-all-start.1) | async-done | bytes 1572896 | tf_op jit(solution)/shard_map/all_to_all | solution.py:79
  254.2 2.5 convert_reduce_fusion.1
  256.7 2.3 gather_fusion.2
  259.0 2.4 gather_fusion.1
  261.3 4.6 convert_subtract_fusion
  268.2 2.3 broadcast_in_dim.92
  270.5 8.8 %all-to-all-start.2 = ((bf16[64,3,4096]{2,1,0:T(4,128)(2,1)}), bf16[64,3,4096]{2,1,0:T(4,128)(2,1)}, u32[]{:S(2)}, u32[]{:S(2)}) async-start(bf16[64,3,4096]{2,1,0:T(4,128)(2,1)} %broadcast_in_dim.92), calls=%async_computation.2 | async-start | bytes 4194304 | tf_op jit(solution)/shard_map/all_to_all | solution.py:87
  279.3 3.1 all_to_all.44
  282.4 3.0 copy.20
  285.4 90.8 %all-to-all-done.2 = bf16[64,3,4096]{2,1,0:T(4,128)(2,1)} async-done(((bf16[64,3,4096]{2,1,0:T(4,128)(2,1)}), bf16[64,3,4096]{2,1,0:T(4,128)(2,1)}, u32[]{:S(2)}, u32[]{:S(2)}) %all-to-all-start.2) | async-done | bytes 1572896 | tf_op jit(solution)/shard_map/all_to_all | solution.py:87
  376.2 4.5 all-to-all-start.4
  380.7 4.3 all_to_all.41
  385.0 2.8 multiply_convert_fusion
  391.2 4.1 all_to_all.42
  395.2 7.0 %all-to-all-done.4 = bf16[192,8,512]{2,0,1:T(8,128)(2,1)S(1)} async-done(((bf16[192,8,512]{2,0,1:T(8,128)(2,1)}), bf16[192,8,512]{2,0,1:T(8,128)(2,1)S(1)}, u32[]{:S(2)}, u32[]{:S(2)}) %all-to-all-start.4) | async-done | bytes 1572896 | tf_op jit(solution)/shard_map/all_to_all | solution.py:98
  402.2 8.9 %all-to-all-start.3 = ((bf16[64,3,4096]{2,1,0:T(4,128)(2,1)}), bf16[64,3,4096]{2,1,0:T(4,128)(2,1)}, u32[]{:S(2)}, u32[]{:S(2)}) async-start(bf16[64,3,4096]{2,1,0:T(4,128)(2,1)} %all_to_all.42), calls=%async_computation.3 | async-start | bytes 4194304 | tf_op jit(solution)/shard_map/all_to_all | solution.py:95
  411.1 13.4 %all_gather.19 = bf16[1536,224]{1,0:T(8,128)(2,1)S(1)} all-gather(bf16[192,224]{1,0:T(8,128)(2,1)S(1)} %get-tuple-element.11), channel_id=1, replica_groups=mesh['dp'=8,'expert'=64] {'dp'}, dimensions={0}, use_global_device_ids=true | all-gather | bytes 774144 | tf_op jit(solution)/shard_map/all_gather | solution.py:103
  426.6 13.6 %all_gather.18 = bf16[1536,224]{1,0:T(8,128)(2,1)S(1)} all-gather(bf16[192,224]{1,0:T(8,128)(2,1)S(1)} %get-tuple-element.12), channel_id=1, replica_groups=mesh['dp'=8,'expert'=64] {'dp'}, dimensions={0}, use_global_device_ids=true | all-gather | bytes 774144 | tf_op jit(solution)/shard_map/all_gather | solution.py:102
  442.3 2.6 reduce_sum.49
  445.9 62.7 %all-to-all-done.3 = bf16[64,3,4096]{2,1,0:T(4,128)(2,1)} async-done(((bf16[64,3,4096]{2,1,0:T(4,128)(2,1)}), bf16[64,3,4096]{2,1,0:T(4,128)(2,1)}, u32[]{:S(2)}, u32[]{:S(2)}) %all-to-all-start.3) | async-done | bytes 1572896 | tf_op jit(solution)/shard_map/all_to_all | solution.py:95
  508.6 2.5 convert_reduce_fusion
  512.2 2.4 gather_fusion.4
  514.6 3.0 add_convert_fusion
  (59 shorter events, 22.3 us)
Async XLA Ops:
  7.2 6.2 %copy-start = (bf16[128,4096]{1,0:T(8,128)(2,1)S(1)}, bf16[128,4096]{1,0:T(8,128)(2,1)}, u32[]{:S(2)}) copy-start(bf16[128,4096]{1,0:T(8,128)(2,1)} %param.7) | copy-start | bytes 3145732
  7.2 127.9 %all-gather.6.cloned.1.call-start = ((), (), s32[]{:S(2)}) async-start(), calls=%async_computation.6 | async-start | bytes 2064384 | tf_op jit(solution)/shard_map/all_gather | solution.py:68
  16.4 116.1 %all-to-all-start = ((bf16[64,3,4096]{2,1,0:T(4,128)(2,1)}), bf16[64,3,4096]{2,1,0:T(4,128)(2,1)S(1)}, u32[]{:S(2)}, u32[]{:S(2)}) async-start(bf16[64,3,4096]{2,1,0:T(4,128)(2,1)} %broadcast_in_dim.87), calls=%async_computation | async-start | bytes 4194304 | tf_op jit(solution)/shard_map/all_to_all | solution.py:64
  35.2 102.6 %all-gather.4.cloned.1.call-start = ((), (), s32[]{:S(2)}) async-start(), calls=%async_computation.5 | async-start | bytes 2064384 | tf_op jit(solution)/shard_map/all_gather | solution.py:67
  35.9 105.2 %all-gather.8.cloned.1.call-start = ((), (), s32[]{:S(2)}) async-start(), calls=%async_computation.7 | async-start | bytes 2064384 | tf_op jit(solution)/shard_map/all_gather | solution.py:69
  148.6 8.6 %copy-start.5 = (f32[128,2]{0,1:T(2,128)S(1)}, f32[128,2]{0,1:T(2,128)}, u32[]{:S(2)}) copy-start(f32[128,2]{0,1:T(2,128)} %param.9) | copy-start | bytes 3076
  148.6 105.6 %all-to-all-start.1 = ((bf16[64,3,4096]{2,1,0:T(4,128)(2,1)}), bf16[64,3,4096]{2,1,0:T(4,128)(2,1)}, u32[]{:S(2)}, u32[]{:S(2)}) async-start(bf16[64,3,4096]{2,1,0:T(4,128)(2,1)} %all_to_all.38), calls=%async_computation.1 | async-start | bytes 4194304 | tf_op jit(solution)/shard_map/all_to_all | solution.py:79
  270.5 105.7 %all-to-all-start.2 = ((bf16[64,3,4096]{2,1,0:T(4,128)(2,1)}), bf16[64,3,4096]{2,1,0:T(4,128)(2,1)}, u32[]{:S(2)}, u32[]{:S(2)}) async-start(bf16[64,3,4096]{2,1,0:T(4,128)(2,1)} %broadcast_in_dim.92), calls=%async_computation.2 | async-start | bytes 4194304 | tf_op jit(solution)/shard_map/all_to_all | solution.py:87
  376.2 26.0 %all-to-all-start.4 = ((bf16[192,8,512]{2,0,1:T(8,128)(2,1)}), bf16[192,8,512]{2,0,1:T(8,128)(2,1)S(1)}, u32[]{:S(2)}, u32[]{:S(2)}) async-start(bf16[192,8,512]{2,0,1:T(8,128)(2,1)} %copy.20), calls=%async_computation.4 | async-start | bytes 3145728 | tf_op jit(solution)/shard_map/all_to_all | solution.py:98
  380.7 4.3 copy-start.4
  385.0 2.8 copy-start.2
  387.9 1.5 copy-start.1
  402.2 106.4 %all-to-all-start.3 = ((bf16[64,3,4096]{2,1,0:T(4,128)(2,1)}), bf16[64,3,4096]{2,1,0:T(4,128)(2,1)}, u32[]{:S(2)}, u32[]{:S(2)}) async-start(bf16[64,3,4096]{2,1,0:T(4,128)(2,1)} %all_to_all.42), calls=%async_computation.3 | async-start | bytes 4194304 | tf_op jit(solution)/shard_map/all_to_all | solution.py:95
  442.3 2.6 copy-start.3
Sparse Core Ops, SparseCore 0:
  10.1 36.9 all-gather.5
  49.2 32.8 all-gather.3
  84.3 32.8 all-gather.7
where the time goes:
time: 525 us; the launch traced here: 524 us
  waiting for transfers between devices  353 us (67%)
  starting transfers between devices  49.6 us (9%)
  local copies, waits for them, and re-layouts  44.5 us (8%)
  blocking collectives  27 us (5%)
  matrix products  18.8 us (4%)
  other arithmetic  17 us (3%)
  between operations  14 us (3%)
    all_to_all x1, waiting for transfers between devices, shards(): lax.all_to_all(outgoing, 'expert', split_axis=0, concat_axis=0, tiled=True)  95.8 us
    all_to_all x1, waiting for transfers between devices, shards(): lax.all_to_all(partial_out, 'expert', split_axis=0, concat_axis=0, tiled=...  94.7 us
    all_to_all x1, waiting for transfers between devices, shards(): lax.all_to_all(outgoing_grad, 'expert', split_axis=0, concat_axis=0, tile...  90.8 us
    all_to_all x1, waiting for transfers between devices, shards(): lax.all_to_all(row_part, 'expert', split_axis=0, concat_axis=0, tiled=True)  62.7 us
    all_to_all x1, starting transfers between devices, shards(): lax.all_to_all(outgoing, 'expert', split_axis=0, concat_axis=0, tiled=True)  18.8 us
    all_gather x1, blocking collectives, shards(): lax.all_gather(grad_gate_pre, 'dp', axis=0, tiled=True)  13.6 us
    all_gather x1, blocking collectives, shards(): lax.all_gather(grad_up_pre, 'dp', axis=0, tiled=True)  13.4 us
  transfers between devices with their start and end apart: 8, of which 5 were waited for; matrix products, arithmetic and copies ran while one was open for 6% of the time, Pallas kernels for 0%

commit v1 on v0

v1 whole, which is shorter than its diff:
```python
import functools

import jax
import jax.numpy as jnp
from jax import lax
from jax.experimental import pallas as pl
from jax.experimental.pallas import tpu as pltpu
from jax.sharding import PartitionSpec as P

MESH = pl.DeviceIdType.MESH
F32, BF16 = jnp.float32, jnp.bfloat16
CAP = 3
NX = 4
NL = 4


def dot_nn(a, b):
    return jnp.dot(a, b, preferred_element_type=F32)


def dot_nt(a, b):
    return lax.dot_general(a, b, (((1,), (1,)), ((), ())), preferred_element_type=F32)


def dot_tn(a, b):
    return lax.dot_general(a, b, (((0,), (0,)), ((), ())), preferred_element_type=F32)


def ds(start, size, unit):
    return pl.ds(pl.multiple_of(start, unit), size)


def layer_kernel(
    nx, nz, ndp, tok_ref, tgt_ref, ids_ref, gv_ref, wg_ref, wu_ref, wd_ref,
    tg_out, gg_out, ug_out,
    wg, wu, wd, fx, fc, p1, p2, xc, gga,
    msg, rmsg, msg2, rmsg2, xs, ts, gs, rg, rows, sel,
    gacc, uacc, hid, ga, ua,
    rx0, rl1, rl0, rx1, rh, s0, s1, tt,
    sems,
):
    nh, ny = nz // NL, ndp // 2
    tok_rows, width = tok_ref.shape
    slots, rall = nz * CAP, nx * nz * CAP
    half = width // 2
    cw = half // nz
    clw = nh * cw
    dsh = width // ndp
    hloc = wg_ref.shape[0]
    hp = gga.shape[2] // 2

    dp, e = lax.axis_index("dp"), lax.axis_index("expert")
    y, c = dp // 2, dp % 2
    x, z = e // nz, e % nz
    r, zh = z % NL, z // NL
    blk = r * nh + zh

    def at_z(k):
        return (dp, x * nz + (z + k + nz) % nz)

    def at_x(k):
        return (dp, (x + k) % nx * nz + z)

    def at_dp(i):
        return (i, e)

    partner = at_dp(y * 2 + 1 - c)
    xrows = ds(x * slots, slots, 16)
    used = [0]

    def send(src, dst, dev):
        n = used[0]
        used[0] += 1
        cp = pltpu.make_async_remote_copy(
            src_ref=src, dst_ref=dst, send_sem=sems.at[0, n], recv_sem=sems.at[1, n],
            device_id=dev, device_id_type=MESH,
        )
        cp.start()
        return cp

    barrier = pltpu.get_barrier_semaphore()
    peers = [at_z(k) for k in range(1, nz)] + [at_x(k) for k in range(1, nx)]
    peers += [at_dp((dp + k) % ndp) for k in range(1, ndp)]
    for dev in peers:
        pl.semaphore_signal(barrier, inc=1, device_id=dev, device_id_type=MESH)
    pl.semaphore_wait(barrier, len(peers))

    def shard_of(i):
        return ds(i * dsh, dsh, 128)

    wsends, wcore = [], []
    for shard, full in ((wg_ref, wg), (wu_ref, wu), (wd_ref, wd)):
        mine = full.at[:, shard_of(dp)]
        wsends.append([send(shard, mine, at_dp((y + k) % ny * 2 + c)) for k in range(1, ny)])
        wcore.append(send(shard, mine, partner))
    for shard, full in ((wg_ref, wg), (wu_ref, wu), (wd_ref, wd)):
        full[:, shard_of(dp)] = shard[...]

    computed0 = ids_ref[0:1, :] < 1
    computed = jnp.logical_or(computed0, ids_ref[1:2, :] < 1)
    live = jnp.where(computed, 1.0, 0.0).astype(F32)
    gate = jnp.where(computed0, gv_ref[0:1, :], gv_ref[1:2, :])
    before = lax.broadcasted_iota(jnp.int32, (tok_rows, tok_rows), 0) < lax.broadcasted_iota(
        jnp.int32, (tok_rows, tok_rows), 1
    )
    live8 = jnp.broadcast_to(live, (8, tok_rows))
    slot = dot_nn(live8.astype(BF16), jnp.where(before, 1.0, 0.0).astype(BF16))
    row8 = lax.broadcasted_iota(jnp.int32, (8, tok_rows), 0).astype(F32)
    selx = jnp.where(slot == row8, live8, 0.0)
    selt = jnp.where(slot == row8 - 3.0, live8, 0.0)
    sel[...] = selx
    gsel = jnp.where(live8 > 0, selx * gate, 0.0)
    g0 = jnp.sum(gsel[0:1], axis=1, keepdims=True)
    g1 = jnp.sum(gsel[1:2], axis=1, keepdims=True)
    g2 = jnp.sum(gsel[2:3], axis=1, keepdims=True)
    rowc = lax.broadcasted_iota(jnp.int32, (8, cw), 0)
    gleft = jnp.where(rowc == 6, g0, jnp.where(rowc == 7, g2, 0.0))
    gright = jnp.where(rowc == 6, g1, 0.0)
    selx, selt = selx.astype(BF16), selt.astype(BF16)
    for k in range(nz):
        col = ((k % NL) * nh + k // NL) * cw
        for h, extra in ((0, gleft), (1, gright)):
            cols = slice(h * half + col, h * half + col + cw)
            piece = dot_nn(selx, tok_ref[:, cols]) + dot_nn(selt, tgt_ref[:, cols])
            msg[k, :, h * cw : (h + 1) * cw] = piece + extra
    rmsg[pl.ds(z, 1)] = msg[pl.ds(z, 1)]
    cps = [send(msg.at[(z + k) % nz], rmsg.at[z], at_z(k)) for k in range(1, nz)]
    for cp in cps:
        cp.wait()
    for k in range(nz):
        b = CAP * k
        xs[b : b + 3, :] = rmsg[k, 0:3, :]
        ts[b : b + 3, :] = rmsg[k, 3:6, :]
        gs[b : b + 1, :] = rmsg[k, 6:7, 0:cw]
        gs[b + 1 : b + 2, :] = rmsg[k, 6:7, cw : 2 * cw]
        gs[b + 2 : b + 3, :] = rmsg[k, 7:8, 0:cw]

    def along_l(ref_of):
        out = []
        for idx, k in enumerate((1, -1)):
            src, dst = ref_of(k, idx, 0, clw)
            out.append(send(src, dst, at_z(k)))
        for k, lo in ((2, 0), (-2, clw // 2)):
            src, dst = ref_of(k, 2, lo, clw // 2)
            out.append(send(src, dst, at_z(k)))
        return out

    def spread1(full):
        out = []
        for k in range(1, nh):
            for h in range(2):
                part = full.at[xrows, ds(h * half + blk * cw, cw, 128)]
                out.append(send(part, part, at_z(NL * k)))
        return out

    def spread2(full):
        def left(k, idx, lo, n):
            part = full.at[xrows, ds(r * clw + lo, n, 128)]
            return part, part

        out = along_l(left)
        part = full.at[xrows, ds(half + r * clw, clw, 128)]
        return out + [send(part, part, at_x(k)) for k in range(1, nx)]

    def spread3(full):
        def right(k, idx, lo, n):
            part = full.at[:, ds(half + r * clw + lo, n, 128)]
            return part, part

        part = full.at[xrows, pl.ds(0, half)]
        out = [send(part, part, at_x(k)) for k in range(1, nx)]
        return out + along_l(right)

    def wait_all(copies):
        for cp in copies:
            cp.wait()

    def fold1(n, part):
        out = []
        for k in range(1, nx):
            theirs = ds((x + k) % nx * slots, slots, 16)
            out.append(send(part.at[theirs, pl.ds(0, half)], rx0.at[n, k - 1], at_x(k)))

        def right(k, idx, lo, size):
            src = part.at[:, ds(half + (r + k + NL) % NL * clw + lo, size, 128)]
            return src, rl1.at[n, idx, :, pl.ds(lo, size)]

        return out + along_l(right)

    def fold2(n, part, copies):
        wait_all(copies)
        for q in range(NL):
            cols = slice(q * clw, (q + 1) * clw)
            total = part[xrows, cols].astype(F32)
            for k in range(nx - 1):
                total += rx0[n, k, :, cols].astype(F32)
            s0[n, :, cols] = total.astype(BF16)
        own = ds(half + r * clw, clw, 128)
        for q in range(nx):
            rws = slice(q * slots, (q + 1) * slots)
            total = part[rws, own].astype(F32)
            for k in range(NL - 1):
                total += rl1[n, k, rws, :].astype(F32)
            s1[n, rws, :] = total.astype(BF16)

        def left(k, idx, lo, size):
            src = s0.at[n, :, ds((r + k + NL) % NL * clw + lo, size, 128)]
            return src, rl0.at[n, idx, :, pl.ds(lo, size)]

        out = along_l(left)
        for k in range(1, nx):
            theirs = ds((x + k) % nx * slots, slots, 16)
            out.append(send(s1.at[n, theirs, :], rx1.at[n, k - 1], at_x(k)))
        return out

    def fold3(n, copies):
        wait_all(copies)
        total = s0[n, :, ds(r * clw, clw, 128)].astype(F32)
        for k in range(NL - 1):
            total += rl0[n, k].astype(F32)
        tt[n, 0] = total.astype(BF16)
        total = s1[n, xrows, :].astype(F32)
        for k in range(nx - 1):
            total += rx1[n, k].astype(F32)
        tt[n, 1] = total.astype(BF16)
        out = []
        for k in range(1, nh):
            for h in range(2):
                src = tt.at[n, h, :, ds((zh + k) % nh * cw, cw, 128)]
                out.append(send(src, rh.at[n, h, k - 1], at_z(NL * k)))
        return out

    def fold4(n, copies):
        wait_all(copies)
        out = []
        for h in range(2):
            total = tt[n, h, :, ds(zh * cw, cw, 128)].astype(F32)
            for k in range(nh - 1):
                total += rh[n, h, k].astype(F32)
            out.append(total)
        return out

    for h in range(2):
        fx[xrows, ds(h * half + blk * cw, cw, 128)] = xs[:, h * cw : (h + 1) * cw].astype(BF16)
    wait_all(spread1(fx))
    wait_all(spread2(fx))
    cps = spread3(fx)
    for sends, full in zip(wsends, (wg, wu, wd)):
        for k, cp in enumerate(sends, 1):
            cp.wait()
            part = full.at[:, shard_of((y - k + ny) % ny * 2 + c)]
            wcore.append(send(part, part, partner))
    wait_all(wcore)
    wait_all(cps)

    xc[dp] = fx[:, shard_of(dp)]
    xcopies = []
    for k in range(1, ndp):
        i = (dp + k) % ndp
        xcopies.append(send(fx.at[:, shard_of(i)], xc.at[dp], at_dp(i)))

    gacc[...] = jnp.zeros_like(gacc)
    uacc[...] = jnp.zeros_like(uacc)

    @pl.loop(0, ndp)
    def _(i):
        cols = shard_of(i)
        block = fx[:, cols]
        gacc[...] += dot_nt(block, wg[:, cols])
        uacc[...] += dot_nt(block, wu[:, cols])

    pre = gacc[...]
    hid[...] = (jax.nn.sigmoid(pre) * pre * uacc[...]).astype(BF16)

    @pl.loop(0, ndp)
    def _(i):
        cols = shard_of(i)
        p1[:, cols] = dot_nn(hid[...], wd[:, cols]).astype(BF16)

    cps = fold1(0, p1)
    cps = fold2(0, p1, cps)
    cps = fold3(0, cps)
    sums = fold4(0, cps)
    for h in range(2):
        weight = gs[...]
        residual = weight * sums[h] - ts[:, h * cw : (h + 1) * cw]
        fc[xrows, ds(h * half + blk * cw, cw, 128)] = (weight * residual).astype(BF16)
    wait_all(spread1(fc))
    wait_all(spread2(fc))
    wait_all(spread3(fc))

    ga[...] = jnp.zeros_like(ga)

    @pl.loop(0, ndp)
    def _(i):
        cols = shard_of(i)
        ga[...] += dot_nt(fc[:, cols], wd[:, cols])

    pre = gacc[...]
    sig = jax.nn.sigmoid(pre)
    grad = ga[...]
    ggv = (grad * uacc[...] * (sig * (1.0 + pre * (1.0 - sig)))).astype(BF16)
    guv = (grad * (sig * pre)).astype(BF16)
    ga[...] = jnp.zeros_like(ga)
    hid[...] = ggv
    ua[...] = guv
    gga[dp] = jnp.zeros((rall, 2 * hp), BF16)
    gga[dp, :, 0:hloc] = ggv
    gga[dp, :, hp : hp + hloc] = guv
    gsends = [send(gga.at[dp], gga.at[dp], at_dp((y + k) % ny * 2 + c)) for k in range(1, ny)]
    gcore = [send(gga.at[dp], gga.at[dp], partner)]

    @pl.loop(0, ndp)
    def _(i):
        cols = shard_of(i)
        p2[:, cols] = (dot_nn(hid[...], wg[:, cols]) + dot_nn(ua[...], wu[:, cols])).astype(BF16)

    cps = fold1(1, p2)
    for k, cp in enumerate(gsends, 1):
        cp.wait()
        i = (y - k + ny) % ny * 2 + c
        gcore.append(send(gga.at[i], gga.at[i], partner))
    cps = fold2(1, p2, cps)
    wait_all(gcore)
    wait_all(xcopies)

    def weight_grad(lo, out_ref):
        def step(i, acc):
            return acc + dot_tn(gga[i, :, lo : lo + hp], xc[i])

        acc = lax.fori_loop(0, ndp, step, jnp.zeros((hp, dsh), F32))
        out_ref[...] = acc[0:hloc].astype(BF16)

    weight_grad(0, gg_out)
    weight_grad(hp, ug_out)
    cps = fold3(1, cps)
    sums = fold4(1, cps)

    rg[slots : slots + 8, :] = jnp.zeros((8, 2 * cw), F32)
    for h in range(2):
        rg[0:slots, h * cw : (h + 1) * cw] = sums[h]
    for k in range(nz):
        msg2[k] = rg[CAP * k : CAP * k + 8, :].astype(BF16)
    rmsg2[pl.ds(z, 1)] = msg2[pl.ds(z, 1)]
    wait_all([send(msg2.at[(z + k) % nz], rmsg2.at[z], at_z(k)) for k in range(1, nz)])
    keep = lax.broadcasted_iota(jnp.int32, (8, cw), 0) < CAP
    for k in range(nz):
        col = ((k % NL) * nh + k // NL) * cw
        for h in range(2):
            value = rmsg2[k, :, h * cw : (h + 1) * cw].astype(F32)
            rows[:, h * half + col : h * half + col + cw] = jnp.where(keep, value, 0.0)

    @pl.loop(0, ndp)
    def _(i):
        cols = shard_of(i)
        tg_out[:, cols] = dot_tn(sel[...].astype(BF16), rows[:, cols].astype(BF16)).astype(BF16)


def shards(nx, ndp, ne, tokens, expert_ids, gate_values, w_gate, w_up, w_down, target):
    tok_rows, width = tokens.shape
    hloc = w_gate.shape[1]
    nz = ne // nx
    nh = nz // NL
    slots, rall = nz * CAP, ne * CAP
    half = width // 2
    cw, dsh = half // nz, width // ndp
    clw = nh * cw
    hp = -(-hloc // 128) * 128
    vmem = pl.BlockSpec(memory_space=pltpu.VMEM)

    def buf(shape, dtype=BF16):
        return pltpu.VMEM(shape, dtype)

    scratch = [
        buf((hloc, width)), buf((hloc, width)), buf((hloc, width)),
        buf((rall, width)), buf((rall, width)), buf((rall, width)), buf((rall, width)),
        buf((ndp, rall, dsh)), buf((ndp, rall, 2 * hp)),
        buf((nz, 8, 2 * cw), F32), buf((nz, 8, 2 * cw), F32),
        buf((nz, 8, 2 * cw)), buf((nz, 8, 2 * cw)),
        buf((slots, 2 * cw), F32), buf((slots, 2 * cw), F32), buf((slots, cw), F32),
        buf((slots + 8, 2 * cw), F32), buf((8, width), F32), buf((8, tok_rows), F32),
        buf((rall, hloc), F32), buf((rall, hloc), F32), buf((rall, hloc)),
        buf((rall, hloc), F32), buf((rall, hloc)),
        buf((2, nx - 1, slots, half)), buf((2, NL - 1, rall, clw)),
        buf((2, NL - 1, slots, clw)), buf((2, nx - 1, slots, clw)),
        buf((2, 2, max(nh - 1, 1), slots, cw)),
        buf((2, slots, half)), buf((2, rall, clw)), buf((2, 2, slots, clw)),
        pltpu.SemaphoreType.DMA((2, 160)),
    ]
    token_grad, gate_grad, up_grad = pl.pallas_call(
        functools.partial(layer_kernel, nx, nz, ndp),
        out_shape=(
            jax.ShapeDtypeStruct((tok_rows, width), BF16),
            jax.ShapeDtypeStruct((hloc, dsh), BF16),
            jax.ShapeDtypeStruct((hloc, dsh), BF16),
        ),
        in_specs=[vmem] * 7,
        out_specs=(vmem,) * 3,
        scratch_shapes=scratch,
        compiler_params=pltpu.CompilerParams(
            collective_id=1, has_side_effects=True, vmem_limit_bytes=60 << 20
        ),
        name="expert_layer",
    )(tokens, target, expert_ids.T, gate_values.T, w_gate.T, w_up.T, w_down)
    return token_grad, gate_grad.T, up_grad.T


def solution(mesh, nx=NX):
    placed = (
        P(("dp", "expert"), None),
        P(("dp", "expert"), None),
        P(("dp", "expert"), None),
        P("dp", "expert"),
        P("dp", "expert"),
        P("expert", "dp"),
        P(("dp", "expert"), None),
    )
    return jax.shard_map(
        functools.partial(shards, nx, mesh.shape["dp"], mesh.shape["expert"]),
        mesh=mesh,
        in_specs=placed,
        out_specs=(P(("dp", "expert"), None), P("dp", "expert"), P("dp", "expert")),
        check_vma=False,
    )
```

time: 525 us -> 149 us (0.28)
  the two profiles are of different devices: /device:TPU:6 before, /device:TPU:32 now
where the time goes in v1:
time: 149 us
  Pallas kernels  144 us (97%)
  local copies, waits for them, and re-layouts  4.04 us (3%)
    pallas_call x1, Pallas kernels, shards(): pl.pallas_call(functools.partial(layer_kernel, nx, nz, ndp), out_shape=(j...  144 us
    unnamed x7, local copies, waits for them, and re-layouts  4.04 us

profile of v1, /device:TPU:32, one launch (start us, length us, event | category | flops | bytes accessed | tf_op | source)
XLA Modules:
  0.0 148.9 jit_solution(14273210694617197233)
XLA Ops:
  0.6 144.2 %expert_layer.1 = (bf16[128,4096]{1,0:T(8,128)(2,1)}, bf16[224,512]{1,0:T(8,128)(2,1)}, bf16[224,512]{1,0:T(8,128)(2,1)}) custom-call(bf16[128,4096]{1,0:T(8,128)(2,1)} %tok_ref.1, bf16[128,4096]{1,0:T(8,128)(2,1)} %tgt_ref.1, s32[2,128]{1,0:T(2,128)} %bitcast.10, f32[2,128]{1,0:T(2,128)} %bitcast.11, bf16[224,512]{1,0:T(8,128)(2,1)} %bitcast.6, ...), custom_call_target="tpu_custom_call" | custom-call | tf_op jit(solution)/shard_map/expert_layer/pallas_call | solution.py:390
  144.8 0.0 copy-start.1
  144.8 2.3 %copy.13 = bf16[128,4096]{1,0:T(8,128)(2,1)} copy(bf16[128,4096]{1,0:T(8,128)(2,1)} %get-tuple-element.12) | data formatting | bytes 2097152
  147.1 0.0 copy-done.1
  147.1 0.0 copy-start
  147.2 0.7 copy.14
  147.8 0.3 copy-done
  148.2 0.7 copy.15
Async XLA Ops:
  144.8 2.3 %copy-start.1 = (bf16[224,512]{1,0:T(8,128)(2,1)S(1)}, bf16[224,512]{1,0:T(8,128)(2,1)}, u32[]{:S(2)}) copy-start(bf16[224,512]{1,0:T(8,128)(2,1)} %get-tuple-element.7) | copy-start | bytes 688132
  147.1 1.0 copy-start

commit v2 on v1

v2 whole, which is shorter than its diff:
```python
import functools

import jax
import jax.numpy as jnp
from jax import lax
from jax.experimental import pallas as pl
from jax.experimental.pallas import tpu as pltpu
from jax.sharding import PartitionSpec as P

MESH = pl.DeviceIdType.MESH
F32, BF16 = jnp.float32, jnp.bfloat16
CAP = 3
NX = 4
NL = 4


def dot_nn(a, b):
    return jnp.dot(a, b, preferred_element_type=F32)


def dot_nt(a, b):
    return lax.dot_general(a, b, (((1,), (1,)), ((), ())), preferred_element_type=F32)


def dot_tn(a, b):
    return lax.dot_general(a, b, (((0,), (0,)), ((), ())), preferred_element_type=F32)


def ds(start, size, unit):
    return pl.ds(pl.multiple_of(start, unit), size)


def layer_kernel(
    nx, nz, ndp, tok_ref, tgt_ref, ids_ref, gv_ref, wg_ref, wu_ref, wd_ref,
    rows_out, sel_out, gg_out, ug_out,
    wg, wu, wd, fx, fc, p1, p2, xc, gga,
    xmsg, xrcv, tmsg, trcv, msg2, rmsg2, xs, ts, gs, rg,
    gacc, uacc, hid, ua,
    rx0, rl1, rl0, rx1, rh, s0, s1, tt,
    sems,
):
    nh, ny = nz // NL, ndp // 2
    tok_rows, width = tok_ref.shape
    slots, rall = nz * CAP, nx * nz * CAP
    half = width // 2
    cw = half // nz
    clw = nh * cw
    dsh = width // ndp
    hloc = wg_ref.shape[0]
    hp = gga.shape[2] // 2

    dp, e = lax.axis_index("dp"), lax.axis_index("expert")
    y, c = dp // 2, dp % 2
    x, z = e // nz, e % nz
    r, zh = z % NL, z // NL
    blk = r * nh + zh

    def at_z(k):
        return (dp, x * nz + (z + k + nz) % nz)

    def at_x(k):
        return (dp, (x + k + nx) % nx * nz + z)

    def at_dp(i):
        return (i, e)

    def at_y(k):
        return (y + k + ny) % ny * 2 + c

    partner = at_dp(y * 2 + 1 - c)

    def rows_of(k):
        return ds((x + k + nx) % nx * slots, slots, 16)

    def class_of(k, h, lo=0, n=None):
        return ds(h * half + (r + k + NL) % NL * clw + lo, clw if n is None else n, 128)

    xrows = rows_of(0)
    used = [0]

    def send(src, dst, dev):
        n = used[0]
        used[0] += 1
        cp = pltpu.make_async_remote_copy(
            src_ref=src, dst_ref=dst, send_sem=sems.at[0, n], recv_sem=sems.at[1, n],
            device_id=dev, device_id_type=MESH,
        )
        cp.start()
        return cp

    def wait_all(copies):
        for cp in copies:
            cp.wait()

    barrier = pltpu.get_barrier_semaphore()
    peers = [at_z(k) for k in range(1, nz)] + [at_x(k) for k in range(1, nx)]
    peers += [at_dp((dp + k) % ndp) for k in range(1, ndp)]
    for dev in peers:
        pl.semaphore_signal(barrier, inc=1, device_id=dev, device_id_type=MESH)

    computed0 = ids_ref[0:1, :] < 1
    computed = jnp.logical_or(computed0, ids_ref[1:2, :] < 1)
    live = jnp.where(computed, 1.0, 0.0).astype(F32)
    gate = jnp.where(computed0, gv_ref[0:1, :], gv_ref[1:2, :])
    before = lax.broadcasted_iota(jnp.int32, (tok_rows, tok_rows), 0) < lax.broadcasted_iota(
        jnp.int32, (tok_rows, tok_rows), 1
    )
    live8 = jnp.broadcast_to(live, (8, tok_rows))
    slot = dot_nn(live8.astype(BF16), jnp.where(before, 1.0, 0.0).astype(BF16))
    row8 = lax.broadcasted_iota(jnp.int32, (8, tok_rows), 0).astype(F32)
    sel = jnp.where(slot == row8, live8, 0.0)
    sel_out[...] = sel
    selx = sel.astype(BF16)
    for k in range(nz):
        col = ((k % NL) * nh + k // NL) * cw
        for h in range(2):
            cols = slice(h * half + col, h * half + col + cw)
            xmsg[k, :, h * cw : (h + 1) * cw] = dot_nn(selx, tok_ref[:, cols]).astype(BF16)
    xrcv[pl.ds(z, 1)] = xmsg[pl.ds(z, 1)]

    pl.semaphore_wait(barrier, len(peers))

    tcps = [send(xmsg.at[(z + k) % nz], xrcv.at[z], at_z(k)) for k in range(1, nz)]

    def shard_of(i):
        return ds(i * dsh, dsh, 128)

    whole = ((wg_ref, wg), (wu_ref, wu), (wd_ref, wd))
    hh = hloc // 2
    wfirst, wrest = [None] * 3, []

    def weight_out(n):
        shard, full = whole[n]
        mine = full.at[:, shard_of(dp)]
        wfirst[n] = [send(shard, mine, at_dp(at_y(k))) for k in ((1, -1) if ny > 2 else (1,))]
        wrest.append(send(shard, mine, partner))

    def weight_on(n):
        full = whole[n][1]
        second = []
        for k, cp in zip((1, -1), wfirst[n]):
            cp.wait()
            cols = shard_of(at_y(-k))
            if ny > 2:
                part = full.at[pl.ds(0 if k == 1 else hh, hh), cols]
                second.append(send(part, part, at_dp(at_y(k))))
            part = full.at[:, cols]
            wrest.append(send(part, part, partner))
        return second

    def weight_end(n, second):
        wait_all(second)
        if ny > 2:
            part = whole[n][1].at[:, shard_of(at_y(2))]
            wrest.append(send(part, part, partner))

    weight_out(0)
    weight_out(1)
    for shard, full in whole:
        full[:, shard_of(dp)] = shard[...]

    gsel = sel * gate
    g0 = jnp.sum(gsel[0:1], axis=1, keepdims=True)
    g1 = jnp.sum(gsel[1:2], axis=1, keepdims=True)
    g2 = jnp.sum(gsel[2:3], axis=1, keepdims=True)
    rowc = lax.broadcasted_iota(jnp.int32, (8, cw), 0)
    gleft = jnp.where(rowc == 3, g0, jnp.where(rowc == 4, g2, 0.0))
    gright = jnp.where(rowc == 3, g1, 0.0)
    keep3 = rowc < CAP
    for k in range(nz):
        col = ((k % NL) * nh + k // NL) * cw
        for h, extra in ((0, gleft), (1, gright)):
            cols = slice(h * half + col, h * half + col + cw)
            piece = dot_nn(selx, tgt_ref[:, cols])
            tmsg[k, :, h * cw : (h + 1) * cw] = jnp.where(keep3, piece, extra)
    trcv[pl.ds(z, 1)] = tmsg[pl.ds(z, 1)]

    def along_l(ref_of):
        out = []
        for idx, k in enumerate((1, -1)):
            src, dst = ref_of(k, idx, 0, clw)
            out.append(send(src, dst, at_z(k)))
        for k, lo in ((2, 0), (-2, clw // 2)):
            src, dst = ref_of(k, 2, lo, clw // 2)
            out.append(send(src, dst, at_z(k)))
        return out

    far = sorted(range(1, nh), key=lambda k: -min(k, nh - k))
    xsteps = list(range(1, nx))

    def spread1(full):
        out = []
        for k in far:
            for h in range(2):
                part = full.at[xrows, ds(h * half + blk * cw, cw, 128)]
                out.append(send(part, part, at_z(NL * k)))
        return out

    def spread2(full, copies):
        wait_all(copies)

        def l_send(rws, h):
            def ref_of(k, idx, lo, n):
                part = full.at[rws, class_of(0, h, lo, n)]
                return part, part

            return along_l(ref_of)

        def x_send(k, h):
            part = full.at[xrows, class_of(k, h)]
            return [send(part, part, at_x(d)) for d in xsteps]

        first = l_send(xrows, 0)
        second = x_send(0, 1)
        last = x_send(0, 0) + l_send(xrows, 1)
        for q in range(3):
            if q < 2:
                first[q].wait()
            else:
                wait_all(first[2:])
            last += x_send((-1, 1, 2)[q], 0)
            if q < nx - 1:
                second[q].wait()
                last += l_send(rows_of(-xsteps[q]), 1)
        return last

    lsteps = (1, -1, 2, 0)
    xorder = xsteps + [0]

    def fold_right(n, part):
        out = []
        for q, d in enumerate(xorder):

            def ref_of(k, idx, lo, size):
                return part.at[rows_of(d), class_of(k, 1, lo, size)], rl1.at[n, q, idx, :, pl.ds(lo, size)]

            out.append(along_l(ref_of))
        return out

    def fold_left(n, part, q):
        cols = class_of(lsteps[q], 0)
        return [send(part.at[rows_of(k), cols], rx0.at[n, k - 1, q], at_x(k)) for k in xsteps]

    def fold2(n, part, left, right):
        out = []
        for q in range(NL):
            if q < nx:
                wait_all(right[q])
                total = part[rows_of(xorder[q]), class_of(0, 1)].astype(F32)
                for k in range(NL - 1):
                    total += rl1[n, q, k].astype(F32)
                s1[n, q] = total.astype(BF16)
                if xorder[q]:
                    out.append(send(s1.at[n, q], rx1.at[n, q], at_x(xorder[q])))
            wait_all(left[q])
            total = part[xrows, class_of(lsteps[q], 0)].astype(F32)
            for k in range(nx - 1):
                total += rx0[n, k, q].astype(F32)
            s0[n, q] = total.astype(BF16)
            if q < 2:
                out.append(send(s0.at[n, q], rl0.at[n, q], at_z(lsteps[q])))
            elif q == 2:
                for k, lo in ((2, 0), (-2, clw // 2)):
                    cols = pl.ds(lo, clw // 2)
                    out.append(send(s0.at[n, q, :, cols], rl0.at[n, q, :, cols], at_z(k)))
        return out

    def fold3(n, copies):
        wait_all(copies)
        total = s0[n, NL - 1].astype(F32)
        for k in range(NL - 1):
            total += rl0[n, k].astype(F32)
        tt[n, 0] = total.astype(BF16)
        total = s1[n, nx - 1].astype(F32)
        for k in range(nx - 1):
            total += rx1[n, k].astype(F32)
        tt[n, 1] = total.astype(BF16)
        out = []
        for k in far:
            for h in range(2):
                src = tt.at[n, h, :, ds((zh + k) % nh * cw, cw, 128)]
                out.append(send(src, rh.at[n, h, k - 1], at_z(NL * k)))
        return out

    def fold4(n, copies):
        wait_all(copies)
        out = []
        for h in range(2):
            total = tt[n, h, :, ds(zh * cw, cw, 128)].astype(F32)
            for k in range(nh - 1):
                total += rh[n, h, k].astype(F32)
            out.append(total)
        return out

    wait_all(tcps)
    for k in range(nz):
        xs[CAP * k : CAP * k + 3, :] = xrcv[k].astype(F32)[0:3]
    for h in range(2):
        fx[xrows, ds(h * half + blk * cw, cw, 128)] = xs[:, h * cw : (h + 1) * cw].astype(BF16)
    cps = spread1(fx)
    second = weight_on(0)
    weight_out(2)
    cps = spread2(fx, cps)
    tcps = [send(tmsg.at[(z + k) % nz], trcv.at[z], at_z(k)) for k in range(1, nz)]
    seconds = [second, weight_on(1)]
    seconds.append(weight_on(2))
    for n in range(3):
        weight_end(n, seconds[n])
    wait_all(cps)
    wait_all(wrest)

    xc[dp] = fx[:, shard_of(dp)]
    xcopies = []
    for k in range(1, ndp):
        i = (dp + k) % ndp
        xcopies.append(send(fx.at[:, shard_of(i)], xc.at[dp], at_dp(i)))

    gacc[...] = dot_nt(fx[...], wg[...])
    uacc[...] = dot_nt(fx[...], wu[...])
    pre = gacc[...]
    hid[...] = (jax.nn.sigmoid(pre) * pre * uacc[...]).astype(BF16)

    def produce(n, part, block):
        for k in lsteps:
            cols = class_of(k, 1)
            part[:, cols] = block(cols).astype(BF16)
        right = fold_right(n, part)
        left = []
        for q, k in enumerate(lsteps):
            cols = class_of(k, 0)
            part[:, cols] = block(cols).astype(BF16)
            left.append(fold_left(n, part, q))
        return left, right

    left, right = produce(0, p1, lambda cols: dot_nn(hid[...], wd[:, cols]))
    wait_all(tcps)
    for k in range(nz):
        b = CAP * k
        ts[b : b + 3, :] = trcv[k, 0:3, :]
        gs[b : b + 1, :] = trcv[k, 3:4, 0:cw]
        gs[b + 1 : b + 2, :] = trcv[k, 3:4, cw : 2 * cw]
        gs[b + 2 : b + 3, :] = trcv[k, 4:5, 0:cw]
    cps = fold2(0, p1, left, right)
    cps = fold3(0, cps)
    sums = fold4(0, cps)
    for h in range(2):
        weight = gs[...]
        residual = weight * sums[h] - ts[:, h * cw : (h + 1) * cw]
        fc[xrows, ds(h * half + blk * cw, cw, 128)] = (weight * residual).astype(BF16)
    cps = spread1(fc)
    cps = spread2(fc, cps)
    wait_all(cps)

    grad = dot_nt(fc[...], wd[...])
    pre = gacc[...]
    sig = jax.nn.sigmoid(pre)
    hid[...] = (grad * uacc[...] * (sig * (1.0 + pre * (1.0 - sig)))).astype(BF16)
    ua[...] = (grad * (sig * pre)).astype(BF16)
    if hp > hloc:
        gga[dp] = jnp.zeros((rall, 2 * hp), BF16)
    gga[dp, :, 0:hloc] = hid[...]
    gga[dp, :, hp : hp + hloc] = ua[...]
    gsends = [send(gga.at[dp], gga.at[dp], at_dp(at_y(k))) for k in range(1, ny)]
    gcore = [send(gga.at[dp], gga.at[dp], partner)]

    left, right = produce(
        1, p2, lambda cols: dot_nn(hid[...], wg[:, cols]) + dot_nn(ua[...], wu[:, cols])
    )
    cps = fold2(1, p2, left, right)
    for k, cp in enumerate(gsends, 1):
        cp.wait()
        i = at_y(-k)
        gcore.append(send(gga.at[i], gga.at[i], partner))
    cps = fold3(1, cps)
    wait_all(gcore)
    wait_all(xcopies)

    cb = min(256, dsh)
    for lo, out_ref in ((0, gg_out), (hp, ug_out)):
        for b in range(0, dsh, cb):
            lhs = gga[:, :, lo : lo + hp].reshape(ndp * rall, hp)
            rhs = xc[:, :, b : b + cb].reshape(ndp * rall, cb)
            out_ref[:, b : b + cb] = dot_tn(lhs, rhs)[0:hloc].astype(BF16)
    sums = fold4(1, cps)

    rg[slots : slots + 8, :] = jnp.zeros((8, 2 * cw), F32)
    for h in range(2):
        rg[0:slots, h * cw : (h + 1) * cw] = sums[h]
    for k in range(nz):
        msg2[k] = rg[CAP * k : CAP * k + 8, :].astype(BF16)
    rmsg2[pl.ds(z, 1)] = msg2[pl.ds(z, 1)]
    wait_all([send(msg2.at[(z + k) % nz], rmsg2.at[z], at_z(k)) for k in range(1, nz)])
    for k in range(nz):
        col = ((k % NL) * nh + k // NL) * cw
        for h in range(2):
            value = rmsg2[k, :, h * cw : (h + 1) * cw].astype(F32)
            value = jnp.where(keep3, value, 0.0)
            rows_out[:, h * half + col : h * half + col + cw] = value.astype(BF16)


def finish_kernel(rows_ref, sel_ref, gg_ref, ug_ref, tg_out, gg_out, ug_out):
    tg_out[...] = dot_tn(sel_ref[...].astype(BF16), rows_ref[...]).astype(BF16)
    gg_out[...] = gg_ref[...]
    ug_out[...] = ug_ref[...]


def shards(nx, ndp, ne, tokens, expert_ids, gate_values, w_gate, w_up, w_down, target):
    tok_rows, width = tokens.shape
    hloc = w_gate.shape[1]
    nz = ne // nx
    nh = nz // NL
    slots, rall = nz * CAP, ne * CAP
    half = width // 2
    cw, dsh = half // nz, width // ndp
    clw = nh * cw
    hp = -(-hloc // 128) * 128
    vmem = pl.BlockSpec(memory_space=pltpu.VMEM)

    def buf(shape, dtype=BF16):
        return pltpu.VMEM(shape, dtype)

    scratch = [
        buf((hloc, width)), buf((hloc, width)), buf((hloc, width)),
        buf((rall, width)), buf((rall, width)), buf((rall, width)), buf((rall, width)),
        buf((ndp, rall, dsh)), buf((ndp, rall, 2 * hp)),
        buf((nz, 8, 2 * cw)), buf((nz, 8, 2 * cw)),
        buf((nz, 8, 2 * cw), F32), buf((nz, 8, 2 * cw), F32),
        buf((nz, 8, 2 * cw)), buf((nz, 8, 2 * cw)),
        buf((slots, 2 * cw), F32), buf((slots, 2 * cw), F32), buf((slots, cw), F32),
        buf((slots + 8, 2 * cw), F32),
        buf((rall, hloc), F32), buf((rall, hloc), F32), buf((rall, hloc)), buf((rall, hloc)),
        buf((2, nx - 1, NL, slots, clw)), buf((2, nx, NL - 1, slots, clw)),
        buf((2, NL - 1, slots, clw)), buf((2, nx - 1, slots, clw)),
        buf((2, 2, max(nh - 1, 1), slots, cw)),
        buf((2, NL, slots, clw)), buf((2, nx, slots, clw)), buf((2, 2, slots, clw)),
        pltpu.SemaphoreType.DMA((2, 320)),
    ]
    shapes = (
        jax.ShapeDtypeStruct((hloc, dsh), BF16),
        jax.ShapeDtypeStruct((hloc, dsh), BF16),
    )
    rows, sel, gate_grad, up_grad = pl.pallas_call(
        functools.partial(layer_kernel, nx, nz, ndp),
        out_shape=(
            jax.ShapeDtypeStruct((8, width), BF16),
            jax.ShapeDtypeStruct((8, tok_rows), F32),
        ) + shapes,
        in_specs=[vmem] * 7,
        out_specs=(vmem,) * 4,
        scratch_shapes=scratch,
        compiler_params=pltpu.CompilerParams(
            collective_id=1, has_side_effects=True, vmem_limit_bytes=60 << 20
        ),
        name="expert_layer",
    )(tokens, target, expert_ids.T, gate_values.T, w_gate.T, w_up.T, w_down)
    token_grad, gate_grad, up_grad = pl.pallas_call(
        finish_kernel,
        out_shape=(jax.ShapeDtypeStruct((tok_rows, width), BF16),) + shapes,
        in_specs=[vmem] * 4,
        out_specs=(vmem,) * 3,
        name="finish",
    )(rows, sel, gate_grad, up_grad)
    return token_grad, gate_grad.T, up_grad.T


def solution(mesh, nx=NX):
    placed = (
        P(("dp", "expert"), None),
        P(("dp", "expert"), None),
        P(("dp", "expert"), None),
        P("dp", "expert"),
        P("dp", "expert"),
        P("expert", "dp"),
        P(("dp", "expert"), None),
    )
    return jax.shard_map(
        functools.partial(shards, nx, mesh.shape["dp"], mesh.shape["expert"]),
        mesh=mesh,
        in_specs=placed,
        out_specs=(P(("dp", "expert"), None), P("dp", "expert"), P("dp", "expert")),
        check_vma=False,
    )
```

time: 149 us -> 137 us (0.919)
  the two profiles are of different devices: /device:TPU:32 before, /device:TPU:16 now
where the time goes in v2:
time: 137 us; the launch traced here: 136 us
  Pallas kernels  136 us (99%)
    pallas_call x1, Pallas kernels, shards(): pl.pallas_call(functools.partial(layer_kernel, nx, nz, ndp), out_shape=(j...  133 us

profile of v2, /device:TPU:16, one launch (start us, length us, event | category | flops | bytes accessed | tf_op | source)
XLA Modules:
  0.0 136.4 jit_solution(2985964779397765032)
XLA Ops:
  0.6 133.2 %expert_layer.1 = (bf16[8,4096]{1,0:T(8,128)(2,1)}, f32[8,128]{1,0:T(8,128)}, bf16[224,512]{1,0:T(8,128)(2,1)}, bf16[224,512]{1,0:T(8,128)(2,1)}) custom-call(bf16[128,4096]{1,0:T(8,128)(2,1)} %tok_ref.1, bf16[128,4096]{1,0:T(8,128)(2,1)} %tgt_ref.1, s32[2,128]{1,0:T(2,128)} %bitcast.8, f32[2,128]{1,0:T(2,128)} %bitcast.9, bf16[224,512]{1,0:T(8,128)(2,1)} %bitcast.6, ...), custom_call_target="tpu_custom_call" | custom-call | tf_op jit(solution)/shard_map/expert_layer/pallas_call | solution.py:442
  133.8 2.6 %finish.1 = (bf16[128,4096]{1,0:T(8,128)(2,1)}, bf16[224,512]{1,0:T(8,128)(2,1)}, bf16[224,512]{1,0:T(8,128)(2,1)}) custom-call(bf16[8,4096]{1,0:T(8,128)(2,1)} %get-tuple-element.10.rows_ref, f32[8,128]{1,0:T(8,128)} %get-tuple-element.11.sel_ref, bf16[224,512]{1,0:T(8,128)(2,1)} %get-tuple-element.12.gg_ref, bf16[224,512]{1,0:T(8,128)(2,1)} %get-tuple-element.13.ug_ref), custom_call_target="tpu_custom_call" | custom-call | tf_op jit(solution)/shard_map/finish/pallas_call | solution.py:456

commit v3 on v2

--- a/solution.py
+++ b/solution.py
@@ -111,16 +111,16 @@
     sel = jnp.where(slot == row8, live8, 0.0)
     sel_out[...] = sel
     selx = sel.astype(BF16)
-    for k in range(nz):
-        col = ((k % NL) * nh + k // NL) * cw
+    for q in range(NL):
         for h in range(2):
-            cols = slice(h * half + col, h * half + col + cw)
-            xmsg[k, :, h * cw : (h + 1) * cw] = dot_nn(selx, tok_ref[:, cols]).astype(BF16)
-    xrcv[pl.ds(z, 1)] = xmsg[pl.ds(z, 1)]
+            cols = slice(h * half + q * clw, h * half + (q + 1) * clw)
+            piece = dot_nn(selx, tok_ref[:, cols])[0:4].astype(BF16)
+            xmsg[q, :, h * clw : (h + 1) * clw] = piece
+    xrcv[pl.ds(z, 1)] = xmsg[pl.ds(r, 1)]
 
     pl.semaphore_wait(barrier, len(peers))
 
-    tcps = [send(xmsg.at[(z + k) % nz], xrcv.at[z], at_z(k)) for k in range(1, nz)]
+    tcps = [send(xmsg.at[(z + k) % NL], xrcv.at[z], at_z(k)) for k in range(1, nz)]
 
     def shard_of(i):
         return ds(i * dsh, dsh, 128)
@@ -196,9 +196,7 @@
                 out.append(send(part, part, at_z(NL * k)))
         return out
 
-    def spread2(full, copies):
-        wait_all(copies)
-
+    def spread2(full, between=()):
         def l_send(rws, h):
             def ref_of(k, idx, lo, n):
                 part = full.at[rws, class_of(0, h, lo, n)]
@@ -214,6 +212,8 @@
         second = x_send(0, 1)
         last = x_send(0, 0) + l_send(xrows, 1)
         for q in range(3):
+            if q < len(between):
+                between[q]()
             if q < 2:
                 first[q].wait()
             else:
@@ -265,16 +265,19 @@
                     out.append(send(s0.at[n, q, :, cols], rl0.at[n, q, :, cols], at_z(k)))
         return out
 
+    def class_sums(n, copies):
+        wait_all(copies)
+        left = s0[n, NL - 1].astype(F32)
+        for k in range(NL - 1):
+            left += rl0[n, k].astype(F32)
+        right = s1[n, nx - 1].astype(F32)
+        for k in range(nx - 1):
+            right += rx1[n, k].astype(F32)
+        return left, right
+
     def fold3(n, copies):
-        wait_all(copies)
-        total = s0[n, NL - 1].astype(F32)
-        for k in range(NL - 1):
-            total += rl0[n, k].astype(F32)
-        tt[n, 0] = total.astype(BF16)
-        total = s1[n, nx - 1].astype(F32)
-        for k in range(nx - 1):
-            total += rx1[n, k].astype(F32)
-        tt[n, 1] = total.astype(BF16)
+        for h, total in enumerate(class_sums(n, copies)):
+            tt[n, h] = total.astype(BF16)
         out = []
         for k in far:
             for h in range(2):
@@ -292,20 +295,24 @@
             out.append(total)
         return out
 
+    seconds = [weight_on(0)]
+    weight_out(2)
     wait_all(tcps)
     for k in range(nz):
         xs[CAP * k : CAP * k + 3, :] = xrcv[k].astype(F32)[0:3]
     for h in range(2):
-        fx[xrows, ds(h * half + blk * cw, cw, 128)] = xs[:, h * cw : (h + 1) * cw].astype(BF16)
-    cps = spread1(fx)
-    second = weight_on(0)
-    weight_out(2)
-    cps = spread2(fx, cps)
+        fx[xrows, class_of(0, h)] = xs[:, h * clw : (h + 1) * clw].astype(BF16)
+    cps = spread2(
+        fx,
+        (
+            lambda: seconds.append(weight_on(1)),
+            lambda: weight_end(0, seconds[0]),
+            lambda: seconds.append(weight_on(2)),
+        ),
+    )
     tcps = [send(tmsg.at[(z + k) % nz], trcv.at[z], at_z(k)) for k in range(1, nz)]
-    seconds = [second, weight_on(1)]
-    seconds.append(weight_on(2))
-    for n in range(3):
-        weight_end(n, seconds[n])
+    weight_end(1, seconds[1])
+    weight_end(2, seconds[2])
     wait_all(cps)
     wait_all(wrest)
 
@@ -347,9 +354,8 @@
         weight = gs[...]
         residual = weight * sums[h] - ts[:, h * cw : (h + 1) * cw]
         fc[xrows, ds(h * half + blk * cw, cw, 128)] = (weight * residual).astype(BF16)
-    cps = spread1(fc)
-    cps = spread2(fc, cps)
-    wait_all(cps)
+    wait_all(spread1(fc))
+    wait_all(spread2(fc))
 
     grad = dot_nt(fc[...], wd[...])
     pre = gacc[...]
@@ -371,7 +377,13 @@
         cp.wait()
         i = at_y(-k)
         gcore.append(send(gga.at[i], gga.at[i], partner))
-    cps = fold3(1, cps)
+    rg[slots : slots + 8, :] = jnp.zeros((8, 2 * clw), F32)
+    for h, total in enumerate(class_sums(1, cps)):
+        rg[0:slots, h * clw : (h + 1) * clw] = total
+    for k in range(nz):
+        msg2[k] = rg[CAP * k : CAP * k + 8, :][0:4].astype(BF16)
+    rmsg2[pl.ds(z, 1)] = msg2[pl.ds(z, 1)]
+    tcps = [send(msg2.at[(z + k) % nz], rmsg2.at[z], at_z(k)) for k in range(1, nz)]
     wait_all(gcore)
     wait_all(xcopies)
 
@@ -381,21 +393,18 @@
             lhs = gga[:, :, lo : lo + hp].reshape(ndp * rall, hp)
             rhs = xc[:, :, b : b + cb].reshape(ndp * rall, cb)
             out_ref[:, b : b + cb] = dot_tn(lhs, rhs)[0:hloc].astype(BF16)
-    sums = fold4(1, cps)
-
-    rg[slots : slots + 8, :] = jnp.zeros((8, 2 * cw), F32)
-    for h in range(2):
-        rg[0:slots, h * cw : (h + 1) * cw] = sums[h]
-    for k in range(nz):
-        msg2[k] = rg[CAP * k : CAP * k + 8, :].astype(BF16)
-    rmsg2[pl.ds(z, 1)] = msg2[pl.ds(z, 1)]
-    wait_all([send(msg2.at[(z + k) % nz], rmsg2.at[z], at_z(k)) for k in range(1, nz)])
-    for k in range(nz):
-        col = ((k % NL) * nh + k // NL) * cw
+
+    wait_all(tcps)
+    keep = lax.broadcasted_iota(jnp.int32, (4, clw), 0) < CAP
+    for q in range(NL):
         for h in range(2):
-            value = rmsg2[k, :, h * cw : (h + 1) * cw].astype(F32)
-            value = jnp.where(keep3, value, 0.0)
-            rows_out[:, h * half + col : h * half + col + cw] = value.astype(BF16)
+            cols = slice(h * clw, (h + 1) * clw)
+            total = rmsg2[q, :, cols].astype(F32)
+            for k in range(1, nh):
+                total += rmsg2[q + NL * k, :, cols].astype(F32)
+            total = jnp.where(keep, total, 0.0)
+            at = h * half + q * clw
+            rows_out[:, at : at + clw] = jnp.concatenate([total, jnp.zeros_like(total)]).astype(BF16)
 
 
 def finish_kernel(rows_ref, sel_ref, gg_ref, ug_ref, tg_out, gg_out, ug_out):
@@ -423,17 +432,17 @@
         buf((hloc, width)), buf((hloc, width)), buf((hloc, width)),
         buf((rall, width)), buf((rall, width)), buf((rall, width)), buf((rall, width)),
         buf((ndp, rall, dsh)), buf((ndp, rall, 2 * hp)),
-        buf((nz, 8, 2 * cw)), buf((nz, 8, 2 * cw)),
+        buf((NL, 4, 2 * clw)), buf((nz, 4, 2 * clw)),
         buf((nz, 8, 2 * cw), F32), buf((nz, 8, 2 * cw), F32),
-        buf((nz, 8, 2 * cw)), buf((nz, 8, 2 * cw)),
-        buf((slots, 2 * cw), F32), buf((slots, 2 * cw), F32), buf((slots, cw), F32),
-        buf((slots + 8, 2 * cw), F32),
+        buf((nz, 4, 2 * clw)), buf((nz, 4, 2 * clw)),
+        buf((slots, 2 * clw), F32), buf((slots, 2 * cw), F32), buf((slots, cw), F32),
+        buf((slots + 8, 2 * clw), F32),
         buf((rall, hloc), F32), buf((rall, hloc), F32), buf((rall, hloc)), buf((rall, hloc)),
         buf((2, nx - 1, NL, slots, clw)), buf((2, nx, NL - 1, slots, clw)),
         buf((2, NL - 1, slots, clw)), buf((2, nx - 1, slots, clw)),
         buf((2, 2, max(nh - 1, 1), slots, cw)),
         buf((2, NL, slots, clw)), buf((2, nx, slots, clw)), buf((2, 2, slots, clw)),
-        pltpu.SemaphoreType.DMA((2, 320)),
+        pltpu.SemaphoreType.DMA((2, 300)),
     ]
     shapes = (
         jax.ShapeDtypeStruct((hloc, dsh), BF16),

time: 137 us -> 120 us (0.88)
  the two profiles are of different devices: /device:TPU:16 before, /device:TPU:6 now
where the time goes in v3:
time: 120 us; the launch traced here: 118 us
  Pallas kernels  117 us (98%)
    pallas_call x1, Pallas kernels, shards(): pl.pallas_call(functools.partial(layer_kernel, nx, nz, ndp), out_shape=(j...  115 us
    pallas_call x1, Pallas kernels, shards(): pl.pallas_call(finish_kernel, out_shape=(jax.ShapeDtypeStruct((tok_rows,...  2.6 us

profile of v3, /device:TPU:6, one launch (start us, length us, event | category | flops | bytes accessed | tf_op | source)
XLA Modules:
  0.0 117.8 jit_solution(12211987145166460948)
XLA Ops:
  0.6 114.5 %expert_layer.1 = (bf16[8,4096]{1,0:T(8,128)(2,1)}, f32[8,128]{1,0:T(8,128)}, bf16[224,512]{1,0:T(8,128)(2,1)}, bf16[224,512]{1,0:T(8,128)(2,1)}) custom-call(bf16[128,4096]{1,0:T(8,128)(2,1)} %tok_ref.1, bf16[128,4096]{1,0:T(8,128)(2,1)} %tgt_ref.1, s32[2,128]{1,0:T(2,128)} %bitcast.8, f32[2,128]{1,0:T(2,128)} %bitcast.9, bf16[224,512]{1,0:T(8,128)(2,1)} %bitcast.6, ...), custom_call_target="tpu_custom_call" | custom-call | tf_op jit(solution)/shard_map/expert_layer/pallas_call | solution.py:451
  115.2 2.6 %finish.1 = (bf16[128,4096]{1,0:T(8,128)(2,1)}, bf16[224,512]{1,0:T(8,128)(2,1)}, bf16[224,512]{1,0:T(8,128)(2,1)}) custom-call(bf16[8,4096]{1,0:T(8,128)(2,1)} %get-tuple-element.10.rows_ref, f32[8,128]{1,0:T(8,128)} %get-tuple-element.11.sel_ref, bf16[224,512]{1,0:T(8,128)(2,1)} %get-tuple-element.12.gg_ref, bf16[224,512]{1,0:T(8,128)(2,1)} %get-tuple-element.13.ug_ref), custom_call_target="tpu_custom_call" | custom-call | tf_op jit(solution)/shard_map/finish/pallas_call | solution.py:465

commit v4 on v3

--- a/solution.py
+++ b/solution.py
@@ -31,13 +31,13 @@
 
 
 def layer_kernel(
-    nx, nz, ndp, tok_ref, tgt_ref, ids_ref, gv_ref, wg_ref, wu_ref, wd_ref,
+    nx, nz, ndp, tok_hbm, tgt_hbm, ids_hbm, gv_hbm, wg_ref, wu_ref, wd_ref,
     rows_out, sel_out, gg_out, ug_out,
     wg, wu, wd, fx, fc, p1, p2, xc, gga,
     xmsg, xrcv, tmsg, trcv, msg2, rmsg2, xs, ts, gs, rg,
     gacc, uacc, hid, ua,
     rx0, rl1, rl0, rx1, rh, s0, s1, tt,
-    sems,
+    tok_ref, tgt_ref, ids_ref, gv_ref, lsems, sems,
 ):
     nh, ny = nz // NL, ndp // 2
     tok_rows, width = tok_ref.shape
@@ -48,12 +48,15 @@
     dsh = width // ndp
     hloc = wg_ref.shape[0]
     hp = gga.shape[2] // 2
+    zfar = sorted(range(1, nz), key=lambda k: -min(k, nz - k))
 
     dp, e = lax.axis_index("dp"), lax.axis_index("expert")
     y, c = dp // 2, dp % 2
     x, z = e // nz, e % nz
     r, zh = z % NL, z // NL
     blk = r * nh + zh
+    near = y * 2 // ny
+    hoff = ((1 - near) * half, near * half)
 
     def at_z(k):
         return (dp, x * nz + (z + k + nz) % nz)
@@ -73,7 +76,7 @@
         return ds((x + k + nx) % nx * slots, slots, 16)
 
     def class_of(k, h, lo=0, n=None):
-        return ds(h * half + (r + k + NL) % NL * clw + lo, clw if n is None else n, 128)
+        return ds(hoff[h] + (r + k + NL) % NL * clw + lo, clw if n is None else n, 128)
 
     xrows = rows_of(0)
     used = [0]
@@ -98,6 +101,20 @@
     for dev in peers:
         pl.semaphore_signal(barrier, inc=1, device_id=dev, device_id_type=MESH)
 
+    def shard_of(i):
+        return ds(i * dsh, dsh, 128)
+
+    pairs = (
+        (ids_hbm, ids_ref), (gv_hbm, gv_ref), (tok_hbm, tok_ref), (tgt_hbm, tgt_ref),
+        (wg_ref, wg.at[:, shard_of(dp)]), (wu_ref, wu.at[:, shard_of(dp)]),
+        (wd_ref, wd.at[:, shard_of(dp)]),
+    )
+    loads = [pltpu.make_async_copy(a, b, lsems.at[n]) for n, (a, b) in enumerate(pairs)]
+    for n in (0, 1, 2, 4, 5, 6, 3):
+        loads[n].start()
+
+    loads[0].wait()
+    loads[1].wait()
     computed0 = ids_ref[0:1, :] < 1
     computed = jnp.logical_or(computed0, ids_ref[1:2, :] < 1)
     live = jnp.where(computed, 1.0, 0.0).astype(F32)
@@ -111,54 +128,51 @@
     sel = jnp.where(slot == row8, live8, 0.0)
     sel_out[...] = sel
     selx = sel.astype(BF16)
+    loads[2].wait()
     for q in range(NL):
         for h in range(2):
-            cols = slice(h * half + q * clw, h * half + (q + 1) * clw)
+            cols = ds(hoff[h] + q * clw, clw, 128)
             piece = dot_nn(selx, tok_ref[:, cols])[0:4].astype(BF16)
             xmsg[q, :, h * clw : (h + 1) * clw] = piece
     xrcv[pl.ds(z, 1)] = xmsg[pl.ds(r, 1)]
 
+    for n in (4, 5, 6):
+        loads[n].wait()
     pl.semaphore_wait(barrier, len(peers))
 
-    tcps = [send(xmsg.at[(z + k) % NL], xrcv.at[z], at_z(k)) for k in range(1, nz)]
-
-    def shard_of(i):
-        return ds(i * dsh, dsh, 128)
-
-    whole = ((wg_ref, wg), (wu_ref, wu), (wd_ref, wd))
+    tcps = [send(xmsg.at[(z + k) % NL], xrcv.at[z], at_z(k)) for k in zfar]
+
+    whole = (wg, wu, wd)
     hh = hloc // 2
-    wfirst, wrest = [None] * 3, []
+    wfirst, wrest = [None] * 3, [[], [], []]
 
     def weight_out(n):
-        shard, full = whole[n]
-        mine = full.at[:, shard_of(dp)]
-        wfirst[n] = [send(shard, mine, at_dp(at_y(k))) for k in ((1, -1) if ny > 2 else (1,))]
-        wrest.append(send(shard, mine, partner))
+        mine = whole[n].at[:, shard_of(dp)]
+        wfirst[n] = [send(mine, mine, at_dp(at_y(k))) for k in ((1, -1) if ny > 2 else (1,))]
+        wrest[n].append(send(mine, mine, partner))
 
     def weight_on(n):
-        full = whole[n][1]
         second = []
         for k, cp in zip((1, -1), wfirst[n]):
             cp.wait()
             cols = shard_of(at_y(-k))
             if ny > 2:
-                part = full.at[pl.ds(0 if k == 1 else hh, hh), cols]
+                part = whole[n].at[pl.ds(0 if k == 1 else hh, hh), cols]
                 second.append(send(part, part, at_dp(at_y(k))))
-            part = full.at[:, cols]
-            wrest.append(send(part, part, partner))
+            part = whole[n].at[:, cols]
+            wrest[n].append(send(part, part, partner))
         return second
 
     def weight_end(n, second):
         wait_all(second)
         if ny > 2:
-            part = whole[n][1].at[:, shard_of(at_y(2))]
-            wrest.append(send(part, part, partner))
+            part = whole[n].at[:, shard_of(at_y(2))]
+            wrest[n].append(send(part, part, partner))
 
     weight_out(0)
     weight_out(1)
-    for shard, full in whole:
-        full[:, shard_of(dp)] = shard[...]
-
+
+    loads[3].wait()
     gsel = sel * gate
     g0 = jnp.sum(gsel[0:1], axis=1, keepdims=True)
     g1 = jnp.sum(gsel[1:2], axis=1, keepdims=True)
@@ -170,7 +184,7 @@
     for k in range(nz):
         col = ((k % NL) * nh + k // NL) * cw
         for h, extra in ((0, gleft), (1, gright)):
-            cols = slice(h * half + col, h * half + col + cw)
+            cols = ds(hoff[h] + col, cw, 128)
             piece = dot_nn(selx, tgt_ref[:, cols])
             tmsg[k, :, h * cw : (h + 1) * cw] = jnp.where(keep3, piece, extra)
     trcv[pl.ds(z, 1)] = tmsg[pl.ds(z, 1)]
@@ -192,7 +206,7 @@
         out = []
         for k in far:
             for h in range(2):
-                part = full.at[xrows, ds(h * half + blk * cw, cw, 128)]
+                part = full.at[xrows, ds(hoff[h] + blk * cw, cw, 128)]
                 out.append(send(part, part, at_z(NL * k)))
         return out
 
@@ -296,25 +310,24 @@
         return out
 
     seconds = [weight_on(0)]
-    weight_out(2)
     wait_all(tcps)
     for k in range(nz):
         xs[CAP * k : CAP * k + 3, :] = xrcv[k].astype(F32)[0:3]
     for h in range(2):
         fx[xrows, class_of(0, h)] = xs[:, h * clw : (h + 1) * clw].astype(BF16)
+
+    def up_then_down():
+        seconds.append(weight_on(1))
+        weight_out(2)
+
     cps = spread2(
         fx,
-        (
-            lambda: seconds.append(weight_on(1)),
-            lambda: weight_end(0, seconds[0]),
-            lambda: seconds.append(weight_on(2)),
-        ),
+        (up_then_down, lambda: weight_end(0, seconds[0]), lambda: weight_end(1, seconds[1])),
     )
-    tcps = [send(tmsg.at[(z + k) % nz], trcv.at[z], at_z(k)) for k in range(1, nz)]
-    weight_end(1, seconds[1])
-    weight_end(2, seconds[2])
+    tcps = [send(tmsg.at[(z + k) % nz], trcv.at[z], at_z(k)) for k in zfar]
+    seconds.append(weight_on(2))
     wait_all(cps)
-    wait_all(wrest)
+    wait_all(wrest[0] + wrest[1])
 
     xc[dp] = fx[:, shard_of(dp)]
     xcopies = []
@@ -327,19 +340,28 @@
     pre = gacc[...]
     hid[...] = (jax.nn.sigmoid(pre) * pre * uacc[...]).astype(BF16)
 
-    def produce(n, part, block):
+    def produce_right(n, part, block):
         for k in lsteps:
             cols = class_of(k, 1)
             part[:, cols] = block(cols).astype(BF16)
-        right = fold_right(n, part)
+        return fold_right(n, part)
+
+    def produce_left(n, part, block):
         left = []
         for q, k in enumerate(lsteps):
             cols = class_of(k, 0)
             part[:, cols] = block(cols).astype(BF16)
             left.append(fold_left(n, part, q))
-        return left, right
-
-    left, right = produce(0, p1, lambda cols: dot_nn(hid[...], wd[:, cols]))
+        return left
+
+    def down(cols):
+        return dot_nn(hid[...], wd[:, cols])
+
+    wait_all(wrest[2])
+    right = produce_right(0, p1, down)
+    weight_end(2, seconds[2])
+    wait_all(wrest[2][3 if ny > 2 else 2 :])
+    left = produce_left(0, p1, down)
     wait_all(tcps)
     for k in range(nz):
         b = CAP * k
@@ -353,7 +375,7 @@
     for h in range(2):
         weight = gs[...]
         residual = weight * sums[h] - ts[:, h * cw : (h + 1) * cw]
-        fc[xrows, ds(h * half + blk * cw, cw, 128)] = (weight * residual).astype(BF16)
+        fc[xrows, ds(hoff[h] + blk * cw, cw, 128)] = (weight * residual).astype(BF16)
     wait_all(spread1(fc))
     wait_all(spread2(fc))
 
@@ -369,9 +391,11 @@
     gsends = [send(gga.at[dp], gga.at[dp], at_dp(at_y(k))) for k in range(1, ny)]
     gcore = [send(gga.at[dp], gga.at[dp], partner)]
 
-    left, right = produce(
-        1, p2, lambda cols: dot_nn(hid[...], wg[:, cols]) + dot_nn(ua[...], wu[:, cols])
-    )
+    def back(cols):
+        return dot_nn(hid[...], wg[:, cols]) + dot_nn(ua[...], wu[:, cols])
+
+    right = produce_right(1, p2, back)
+    left = produce_left(1, p2, back)
     cps = fold2(1, p2, left, right)
     for k, cp in enumerate(gsends, 1):
         cp.wait()
@@ -383,7 +407,7 @@
     for k in range(nz):
         msg2[k] = rg[CAP * k : CAP * k + 8, :][0:4].astype(BF16)
     rmsg2[pl.ds(z, 1)] = msg2[pl.ds(z, 1)]
-    tcps = [send(msg2.at[(z + k) % nz], rmsg2.at[z], at_z(k)) for k in range(1, nz)]
+    tcps = [send(msg2.at[(z + k) % nz], rmsg2.at[z], at_z(k)) for k in zfar]
     wait_all(gcore)
     wait_all(xcopies)
 
@@ -403,8 +427,7 @@
             for k in range(1, nh):
                 total += rmsg2[q + NL * k, :, cols].astype(F32)
             total = jnp.where(keep, total, 0.0)
-            at = h * half + q * clw
-            rows_out[:, at : at + clw] = jnp.concatenate([total, jnp.zeros_like(total)]).astype(BF16)
+            rows_out[:, ds(hoff[h] + q * clw, clw, 128)] = jnp.concatenate([total, jnp.zeros_like(total)]).astype(BF16)
 
 
 def finish_kernel(rows_ref, sel_ref, gg_ref, ug_ref, tg_out, gg_out, ug_out):
@@ -442,6 +465,9 @@
         buf((2, NL - 1, slots, clw)), buf((2, nx - 1, slots, clw)),
         buf((2, 2, max(nh - 1, 1), slots, cw)),
         buf((2, NL, slots, clw)), buf((2, nx, slots, clw)), buf((2, 2, slots, clw)),
+        buf((tok_rows, width)), buf((tok_rows, width)),
+        buf((2, tok_rows), jnp.int32), buf((2, tok_rows), F32),
+        pltpu.SemaphoreType.DMA((7,)),
         pltpu.SemaphoreType.DMA((2, 300)),
     ]
     shapes = (
@@ -454,7 +480,7 @@
             jax.ShapeDtypeStruct((8, width), BF16),
             jax.ShapeDtypeStruct((8, tok_rows), F32),
         ) + shapes,
-        in_specs=[vmem] * 7,
+        in_specs=[pl.BlockSpec(memory_space=pl.ANY)] * 7,
         out_specs=(vmem,) * 4,
         scratch_shapes=scratch,
         compiler_params=pltpu.CompilerParams(

time: 120 us -> 126 us (1.050)
  the two profiles are of different devices: /device:TPU:6 before, /device:TPU:24 now
where the time goes in v4:
time: 126 us
  Pallas kernels  126 us (100%)
    pallas_call x1, Pallas kernels, shards(): pl.pallas_call(functools.partial(layer_kernel, nx, nz, ndp), out_shape=(j...  123 us
    pallas_call x1, Pallas kernels, shards(): pl.pallas_call(finish_kernel, out_shape=(jax.ShapeDtypeStruct((tok_rows,...  2.6 us

profile of v4, /device:TPU:24, one launch (start us, length us, event | category | flops | bytes accessed | tf_op | source)
XLA Modules:
  0.0 126.2 jit_solution(2873198192449348785)
XLA Ops:
  0.6 123.0 %expert_layer.1 = (bf16[8,4096]{1,0:T(8,128)(2,1)}, f32[8,128]{1,0:T(8,128)}, bf16[224,512]{1,0:T(8,128)(2,1)}, bf16[224,512]{1,0:T(8,128)(2,1)}) custom-call(bf16[128,4096]{1,0:T(8,128)(2,1)} %tok_hbm.1, bf16[128,4096]{1,0:T(8,128)(2,1)} %tgt_hbm.1, s32[2,128]{1,0:T(2,128)} %bitcast.8, f32[2,128]{1,0:T(2,128)} %bitcast.9, bf16[224,512]{1,0:T(8,128)(2,1)} %bitcast.6, ...), custom_call_target="tpu_custom_call" | custom-call | tf_op jit(solution)/shard_map/expert_layer/pallas_call | solution.py:477
  123.6 2.6 %finish.1 = (bf16[128,4096]{1,0:T(8,128)(2,1)}, bf16[224,512]{1,0:T(8,128)(2,1)}, bf16[224,512]{1,0:T(8,128)(2,1)}) custom-call(bf16[8,4096]{1,0:T(8,128)(2,1)} %get-tuple-element.10.rows_ref, f32[8,128]{1,0:T(8,128)} %get-tuple-element.11.sel_ref, bf16[224,512]{1,0:T(8,128)(2,1)} %get-tuple-element.12.gg_ref, bf16[224,512]{1,0:T(8,128)(2,1)} %get-tuple-element.13.ug_ref), custom_call_target="tpu_custom_call" | custom-call | tf_op jit(solution)/shard_map/finish/pallas_call | solution.py:491

commit v5 on v4

--- a/solution.py
+++ b/solution.py
@@ -310,6 +310,7 @@
         return out
 
     seconds = [weight_on(0)]
+    weight_out(2)
     wait_all(tcps)
     for k in range(nz):
         xs[CAP * k : CAP * k + 3, :] = xrcv[k].astype(F32)[0:3]
@@ -318,23 +319,17 @@
 
     def up_then_down():
         seconds.append(weight_on(1))
-        weight_out(2)
 
     cps = spread2(
         fx,
-        (up_then_down, lambda: weight_end(0, seconds[0]), lambda: weight_end(1, seconds[1])),
+        (up_then_down, lambda: weight_end(0, seconds[0]), lambda: seconds.append(weight_on(2))),
     )
     tcps = [send(tmsg.at[(z + k) % nz], trcv.at[z], at_z(k)) for k in zfar]
-    seconds.append(weight_on(2))
+    weight_end(1, seconds[1])
     wait_all(cps)
     wait_all(wrest[0] + wrest[1])
 
     xc[dp] = fx[:, shard_of(dp)]
-    xcopies = []
-    for k in range(1, ndp):
-        i = (dp + k) % ndp
-        xcopies.append(send(fx.at[:, shard_of(i)], xc.at[dp], at_dp(i)))
-
     gacc[...] = dot_nt(fx[...], wg[...])
     uacc[...] = dot_nt(fx[...], wu[...])
     pre = gacc[...]
@@ -362,6 +357,10 @@
     weight_end(2, seconds[2])
     wait_all(wrest[2][3 if ny > 2 else 2 :])
     left = produce_left(0, p1, down)
+    xcopies = []
+    for k in range(1, ndp):
+        i = (dp + k) % ndp
+        xcopies.append(send(fx.at[:, shard_of(i)], xc.at[dp], at_dp(i)))
     wait_all(tcps)
     for k in range(nz):
         b = CAP * k

time: 126 us -> 120 us (0.952)
  the two profiles are of different devices: /device:TPU:24 before, /device:TPU:6 now
where the time goes in v5:
time: 120 us; the launch traced here: 119 us
  Pallas kernels  118 us (98%)
    pallas_call x1, Pallas kernels, shards(): pl.pallas_call(functools.partial(layer_kernel, nx, nz, ndp), out_shape=(j...  115 us
    pallas_call x1, Pallas kernels, shards(): pl.pallas_call(finish_kernel, out_shape=(jax.ShapeDtypeStruct((tok_rows,...  2.61 us

profile of v5, /device:TPU:6, one launch (start us, length us, event | category | flops | bytes accessed | tf_op | source)
XLA Modules:
  0.0 118.7 jit_solution(16149342801579862827)
XLA Ops:
  0.6 115.4 %expert_layer.1 = (bf16[8,4096]{1,0:T(8,128)(2,1)}, f32[8,128]{1,0:T(8,128)}, bf16[224,512]{1,0:T(8,128)(2,1)}, bf16[224,512]{1,0:T(8,128)(2,1)}) custom-call(bf16[128,4096]{1,0:T(8,128)(2,1)} %tok_hbm.1, bf16[128,4096]{1,0:T(8,128)(2,1)} %tgt_hbm.1, s32[2,128]{1,0:T(2,128)} %bitcast.8, f32[2,128]{1,0:T(2,128)} %bitcast.9, bf16[224,512]{1,0:T(8,128)(2,1)} %bitcast.6, ...), custom_call_target="tpu_custom_call" | custom-call | tf_op jit(solution)/shard_map/expert_layer/pallas_call | solution.py:476
  116.1 2.6 %finish.1 = (bf16[128,4096]{1,0:T(8,128)(2,1)}, bf16[224,512]{1,0:T(8,128)(2,1)}, bf16[224,512]{1,0:T(8,128)(2,1)}) custom-call(bf16[8,4096]{1,0:T(8,128)(2,1)} %get-tuple-element.10.rows_ref, f32[8,128]{1,0:T(8,128)} %get-tuple-element.11.sel_ref, bf16[224,512]{1,0:T(8,128)(2,1)} %get-tuple-element.12.gg_ref, bf16[224,512]{1,0:T(8,128)(2,1)} %get-tuple-element.13.ug_ref), custom_call_target="tpu_custom_call" | custom-call | tf_op jit(solution)/shard_map/finish/pallas_call | solution.py:490

commit v6 on v4

--- a/solution.py
+++ b/solution.py
@@ -310,6 +310,7 @@
         return out
 
     seconds = [weight_on(0)]
+    weight_out(2)
     wait_all(tcps)
     for k in range(nz):
         xs[CAP * k : CAP * k + 3, :] = xrcv[k].astype(F32)[0:3]
@@ -318,14 +319,14 @@
 
     def up_then_down():
         seconds.append(weight_on(1))
-        weight_out(2)
 
     cps = spread2(
         fx,
-        (up_then_down, lambda: weight_end(0, seconds[0]), lambda: weight_end(1, seconds[1])),
+        (up_then_down, lambda: weight_end(0, seconds[0]), lambda: seconds.append(weight_on(2))),
     )
     tcps = [send(tmsg.at[(z + k) % nz], trcv.at[z], at_z(k)) for k in zfar]
-    seconds.append(weight_on(2))
+    weight_end(1, seconds[1])
+    weight_end(2, seconds[2])
     wait_all(cps)
     wait_all(wrest[0] + wrest[1])
 
@@ -359,8 +360,6 @@
 
     wait_all(wrest[2])
     right = produce_right(0, p1, down)
-    weight_end(2, seconds[2])
-    wait_all(wrest[2][3 if ny > 2 else 2 :])
     left = produce_left(0, p1, down)
     wait_all(tcps)
     for k in range(nz):

time: 126 us -> 121 us (0.960)
  the two profiles are of different devices: /device:TPU:24 before, /device:TPU:6 now
where the time goes in v6:
time: 121 us; the launch traced here: 119 us
  Pallas kernels  118 us (98%)
    pallas_call x1, Pallas kernels, shards(): pl.pallas_call(functools.partial(layer_kernel, nx, nz, ndp), out_shape=(j...  116 us
    pallas_call x1, Pallas kernels, shards(): pl.pallas_call(finish_kernel, out_shape=(jax.ShapeDtypeStruct((tok_rows,...  2.61 us

profile of v6, /device:TPU:6, one launch (start us, length us, event | category | flops | bytes accessed | tf_op | source)
XLA Modules:
  0.0 119.1 jit_solution(16614823848901477801)
XLA Ops:
  0.6 115.8 %expert_layer.1 = (bf16[8,4096]{1,0:T(8,128)(2,1)}, f32[8,128]{1,0:T(8,128)}, bf16[224,512]{1,0:T(8,128)(2,1)}, bf16[224,512]{1,0:T(8,128)(2,1)}) custom-call(bf16[128,4096]{1,0:T(8,128)(2,1)} %tok_hbm.1, bf16[128,4096]{1,0:T(8,128)(2,1)} %tgt_hbm.1, s32[2,128]{1,0:T(2,128)} %bitcast.8, f32[2,128]{1,0:T(2,128)} %bitcast.9, bf16[224,512]{1,0:T(8,128)(2,1)} %bitcast.6, ...), custom_call_target="tpu_custom_call" | custom-call | tf_op jit(solution)/shard_map/expert_layer/pallas_call | solution.py:476
  116.5 2.6 %finish.1 = (bf16[128,4096]{1,0:T(8,128)(2,1)}, bf16[224,512]{1,0:T(8,128)(2,1)}, bf16[224,512]{1,0:T(8,128)(2,1)}) custom-call(bf16[8,4096]{1,0:T(8,128)(2,1)} %get-tuple-element.10.rows_ref, f32[8,128]{1,0:T(8,128)} %get-tuple-element.11.sel_ref, bf16[224,512]{1,0:T(8,128)(2,1)} %get-tuple-element.12.gg_ref, bf16[224,512]{1,0:T(8,128)(2,1)} %get-tuple-element.13.ug_ref), custom_call_target="tpu_custom_call" | custom-call | tf_op jit(solution)/shard_map/finish/pallas_call | solution.py:490

commit v7 on v6

--- a/solution.py
+++ b/solution.py
@@ -110,8 +110,41 @@
         (wd_ref, wd.at[:, shard_of(dp)]),
     )
     loads = [pltpu.make_async_copy(a, b, lsems.at[n]) for n, (a, b) in enumerate(pairs)]
-    for n in (0, 1, 2, 4, 5, 6, 3):
+    for n in (4, 5, 6, 0, 1, 2, 3):
         loads[n].start()
+    for n in (4, 5, 6):
+        loads[n].wait()
+    pl.semaphore_wait(barrier, len(peers))
+
+    whole = (wg, wu, wd)
+    hh = hloc // 2
+    wfirst, wrest = [None] * 3, [[], [], []]
+
+    def weight_out(n):
+        mine = whole[n].at[:, shard_of(dp)]
+        wfirst[n] = [send(mine, mine, at_dp(at_y(k))) for k in ((1, -1) if ny > 2 else (1,))]
+        wrest[n].append(send(mine, mine, partner))
+
+    def weight_on(n):
+        second = []
+        for k, cp in zip((1, -1), wfirst[n]):
+            cp.wait()
+            cols = shard_of(at_y(-k))
+            if ny > 2:
+                part = whole[n].at[pl.ds(0 if k == 1 else hh, hh), cols]
+                second.append(send(part, part, at_dp(at_y(k))))
+            part = whole[n].at[:, cols]
+            wrest[n].append(send(part, part, partner))
+        return second
+
+    def weight_end(n, second):
+        wait_all(second)
+        if ny > 2:
+            part = whole[n].at[:, shard_of(at_y(2))]
+            wrest[n].append(send(part, part, partner))
+
+    weight_out(0)
+    weight_out(1)
 
     loads[0].wait()
     loads[1].wait()
@@ -136,41 +169,7 @@
             xmsg[q, :, h * clw : (h + 1) * clw] = piece
     xrcv[pl.ds(z, 1)] = xmsg[pl.ds(r, 1)]
 
-    for n in (4, 5, 6):
-        loads[n].wait()
-    pl.semaphore_wait(barrier, len(peers))
-
     tcps = [send(xmsg.at[(z + k) % NL], xrcv.at[z], at_z(k)) for k in zfar]
-
-    whole = (wg, wu, wd)
-    hh = hloc // 2
-    wfirst, wrest = [None] * 3, [[], [], []]
-
-    def weight_out(n):
-        mine = whole[n].at[:, shard_of(dp)]
-        wfirst[n] = [send(mine, mine, at_dp(at_y(k))) for k in ((1, -1) if ny > 2 else (1,))]
-        wrest[n].append(send(mine, mine, partner))
-
-    def weight_on(n):
-        second = []
-        for k, cp in zip((1, -1), wfirst[n]):
-            cp.wait()
-            cols = shard_of(at_y(-k))
-            if ny > 2:
-                part = whole[n].at[pl.ds(0 if k == 1 else hh, hh), cols]
-                second.append(send(part, part, at_dp(at_y(k))))
-            part = whole[n].at[:, cols]
-            wrest[n].append(send(part, part, partner))
-        return second
-
-    def weight_end(n, second):
-        wait_all(second)
-        if ny > 2:
-            part = whole[n].at[:, shard_of(at_y(2))]
-            wrest[n].append(send(part, part, partner))
-
-    weight_out(0)
-    weight_out(1)
 
     loads[3].wait()
     gsel = sel * gate

time: 121 us -> 120 us (level)
    pallas_call x1, Pallas kernels: 116 us -> 115 us  [shards(): pl.pallas_call(functools.partial(layer_kernel, nx, nz, ndp), out_shape=(j...]
where the time goes in v7:
time: 120 us; the launch traced here: 118 us
  Pallas kernels  117 us (98%)
    pallas_call x1, Pallas kernels, shards(): pl.pallas_call(functools.partial(layer_kernel, nx, nz, ndp), out_shape=(j...  115 us
    pallas_call x1, Pallas kernels, shards(): pl.pallas_call(finish_kernel, out_shape=(jax.ShapeDtypeStruct((tok_rows,...  2.61 us

profile of v7, /device:TPU:6, one launch (start us, length us, event | category | flops | bytes accessed | tf_op | source)
XLA Modules:
  0.0 117.8 jit_solution(1221290429188371043)
XLA Ops:
  0.6 114.6 %expert_layer.1 = (bf16[8,4096]{1,0:T(8,128)(2,1)}, f32[8,128]{1,0:T(8,128)}, bf16[224,512]{1,0:T(8,128)(2,1)}, bf16[224,512]{1,0:T(8,128)(2,1)}) custom-call(bf16[128,4096]{1,0:T(8,128)(2,1)} %tok_hbm.1, bf16[128,4096]{1,0:T(8,128)(2,1)} %tgt_hbm.1, s32[2,128]{1,0:T(2,128)} %bitcast.8, f32[2,128]{1,0:T(2,128)} %bitcast.9, bf16[224,512]{1,0:T(8,128)(2,1)} %bitcast.6, ...), custom_call_target="tpu_custom_call" | custom-call | tf_op jit(solution)/shard_map/expert_layer/pallas_call | solution.py:475
  115.2 2.6 %finish.1 = (bf16[128,4096]{1,0:T(8,128)(2,1)}, bf16[224,512]{1,0:T(8,128)(2,1)}, bf16[224,512]{1,0:T(8,128)(2,1)}) custom-call(bf16[8,4096]{1,0:T(8,128)(2,1)} %get-tuple-element.10.rows_ref, f32[8,128]{1,0:T(8,128)} %get-tuple-element.11.sel_ref, bf16[224,512]{1,0:T(8,128)(2,1)} %get-tuple-element.12.gg_ref, bf16[224,512]{1,0:T(8,128)(2,1)} %get-tuple-element.13.ug_ref), custom_call_target="tpu_custom_call" | custom-call | tf_op jit(solution)/shard_map/finish/pallas_call | solution.py:489
